TPU v7x, 512 devices: a whole 4x4x16 slice. The times are simulated.
512 devices in a mesh: ctx: 64 (over z_hi, x, y, core), pair: 8 (over z_lo).
Axes of the slice: x: 4, y: 4, z: 16 (z_hi: 2, z_lo: 8; z = z_hi * 8 + z_lo), core: 2. Of those that a mesh axis runs over, the one named last changes fastest.
Arguments:
- tokens: bfloat16 [8, 8192, 1536], P('pair', 'ctx'), may hold values from -24 to 24
- w_query: bfloat16 [1536, 512], P('pair'), may hold values from -0.15625 to 0.15625
- w_key: bfloat16 [1536, 128], P('pair'), may hold values from -0.15625 to 0.15625
- w_value: bfloat16 [1536, 192], P('pair'), may hold values from -0.15625 to 0.15625
- w_out: bfloat16 [768, 1536], P('pair'), may hold values from -0.21875 to 0.21875
- norm_gain: float32 [1536], replicated, may hold values from 0.5 to 1.5
- w_pair: bfloat16 [1536, 256], replicated, may hold values from -0.15625 to 0.15625
- conv_weight: bfloat16 [9, 128, 128], replicated, may hold values from -0.1875 to 0.1875
Outputs:
- seq_out: bfloat16 [8, 8192, 1536], P('pair', 'ctx')
- pair_out: bfloat16 [8, 512, 512, 128], P(None, 'ctx', 'pair')
All inputs are finite; a program needn't handle non-finite values.
Results may differ from a plain program's by a relative error of at most 0.014.
The roundings to bfloat16 on the way count: a program that leaves them out, or rounds other values in their place, can miss the bound.
Values may be sent and summed in bfloat16 or wider, within the bound.
A program may use at most 128 MiB of HBM per device.

v0:
```python
import jax
import jax.numpy as jnp
from jax import lax
from jax.sharding import PartitionSpec as P

H = 4
KEY = 128
VAL = 192
PC = 128
POOL = 16
DILATION_STEP = 2


def with_halo(cells, sides, width):
    for axis, dim in sides:
        count = lax.axis_size(axis)
        ends = count - 1
        head = lax.slice_in_dim(cells, 0, width, axis=dim)
        tail = lax.slice_in_dim(cells, cells.shape[dim] - width, cells.shape[dim], axis=dim)
        cells = jnp.concatenate(
            [
                lax.ppermute(tail, axis, [(i, (i + 1) % count) for i in range(ends)]),
                cells,
                lax.ppermute(head, axis, [((i + 1) % count, i) for i in range(ends)]),
            ],
            axis=dim,
        )
    return cells


def on_device(tokens, w_query, w_key, w_value, w_out, norm_gain, w_pair, conv_weight):
    seq_block, row_count, width = tokens.shape
    flat = tokens.reshape(seq_block * row_count, width)
    pieces = (
        lax.all_gather(w_query, "pair", axis=0, tiled=True),
        lax.all_gather(w_key, "pair", axis=0, tiled=True),
        lax.all_gather(w_value, "pair", axis=0, tiled=True),
    )
    columns = flat
    queries, keys, values = tuple(
        (jnp.dot(columns, piece_item, preferred_element_type=jnp.float32) for piece_item in pieces)
    )
    queries = queries.astype(jnp.bfloat16).reshape(seq_block, row_count, H, KEY)
    keys = keys.astype(jnp.bfloat16).reshape(seq_block, row_count, KEY)
    values = values.astype(jnp.bfloat16).reshape(seq_block, row_count, VAL)
    scaling = KEY ** (-0.5)
    highest = jnp.full((seq_block, H, row_count), -1e30, jnp.float32)
    key_piece = lax.all_gather(keys, "ctx", axis=1, tiled=True)
    value_piece = lax.all_gather(values, "ctx", axis=1, tiled=True)
    scores = (
        jnp.einsum("bqhk,bnk->bhqn", queries, key_piece, preferred_element_type=jnp.float32)
        * scaling
    )
    new_high = jnp.maximum(highest, jnp.max(scores, axis=-1))
    weights = jnp.exp(scores - new_high[..., None])
    totals = jnp.sum(weights, axis=-1)
    accum = jnp.einsum(
        "bhqn,bnv->bhqv",
        weights.astype(jnp.bfloat16),
        value_piece,
        preferred_element_type=jnp.float32,
    )
    running = (new_high, totals, accum)
    highest, totals, accum = running
    mixed = (accum / totals[..., None]).astype(jnp.bfloat16)
    mixed = jnp.transpose(mixed, (0, 2, 1, 3)).reshape(seq_block * row_count, H * VAL)
    columns = mixed
    projected = jnp.dot(
        columns,
        lax.all_gather(w_out, "pair", axis=0, tiled=True),
        preferred_element_type=jnp.float32,
    )
    summed = tokens.astype(jnp.float32) + projected.reshape(seq_block, row_count, width)
    seq_out = summed.astype(jnp.bfloat16)
    pooled = jnp.mean(summed.reshape(seq_block, row_count // POOL, POOL, width), axis=2)
    normed = (
        pooled * lax.rsqrt(jnp.mean(pooled * pooled, axis=-1, keepdims=True) + 1e-06) * norm_gain
    )
    normed = normed.astype(jnp.bfloat16)
    averaged_rows = row_count // POOL
    both = jnp.dot(
        normed.reshape(seq_block * averaged_rows, width), w_pair, preferred_element_type=jnp.float32
    ).astype(jnp.bfloat16)
    both = both.reshape(seq_block, averaged_rows, 2 * PC)
    rowpart = both[:, :, :PC]
    colpart = both[:, :, PC:]
    rows_all = lax.all_gather(rowpart, "pair", axis=0, tiled=True)
    ctx_count = lax.axis_size("ctx")
    pair_count = lax.axis_size("pair")
    map_len = averaged_rows * ctx_count
    column_total = map_len // pair_count
    gathered = lax.all_gather(colpart, ("ctx", "pair"), axis=1, tiled=True)
    gathered = gathered.reshape(seq_block, ctx_count, pair_count, averaged_rows, PC)
    gathered = jnp.transpose(gathered, (2, 0, 1, 3, 4)).reshape(pair_count * seq_block, map_len, PC)
    cols_all = lax.dynamic_slice_in_dim(
        gathered, lax.axis_index("pair") * column_total, column_total, 1
    )
    pairwise_grid = (
        rows_all.astype(jnp.float32)[:, :, None, :] * cols_all.astype(jnp.float32)[:, None, :, :]
    ).astype(jnp.bfloat16)
    padded_map = with_halo(pairwise_grid, (("ctx", 1), ("pair", 2)), DILATION_STEP)
    seq_total = pairwise_grid.shape[0]
    cells = seq_total * averaged_rows * column_total
    total = jnp.zeros((cells, PC), jnp.float32)
    for row_offset in range(3):
        for column_offset in range(3):
            kernel_window = padded_map[
                :,
                row_offset * DILATION_STEP : row_offset * DILATION_STEP + averaged_rows,
                column_offset * DILATION_STEP : column_offset * DILATION_STEP + column_total,
                :,
            ]
            total = total + jnp.dot(
                kernel_window.reshape(cells, PC),
                conv_weight[row_offset * 3 + column_offset],
                preferred_element_type=jnp.float32,
            )
    result = pairwise_grid.astype(jnp.float32) + jax.nn.gelu(
        total.reshape(seq_total, averaged_rows, column_total, PC)
    )
    return (seq_out, result.astype(jnp.bfloat16))


def solution(mesh):
    return jax.shard_map(
        on_device,
        mesh=mesh,
        in_specs=(
            P("pair", "ctx", None),
            P("pair", None),
            P("pair", None),
            P("pair", None),
            P("pair", None),
            P(),
            P(),
            P(),
        ),
        out_specs=(P("pair", "ctx", None), P(None, "ctx", "pair", None)),
        check_vma=False,
    )
```

profile of v0, /device:TPU:1, one launch (start us, length us, event | category | flops | bytes accessed | tf_op | source)
XLA Modules:
  0.0 1492.8 jit_solution(11475428438196550576)
XLA Ops:
  7.2 0.0 all-gather.8.cloned.1.call-start
  7.2 0.7 all-gather.8.cloned.1.call-update
  7.9 0.0 all-gather.14.cloned.1.call-start
  8.0 46.9 %all_gather.24 = bf16[1536,128]{1,0:T(8,128)(2,1)S(1)} all-gather(bf16[192,128]{1,0:T(8,128)(2,1)} %param.10), channel_id=1, replica_groups=mesh['ctx'=64,'pair'=8] {'pair'}, dimensions={0}, use_global_device_ids=true | all-gather | bytes 442368 | tf_op jit(solution)/shard_map/all_gather | solution.py:36
  54.9 1.9 convolution_convert_fusion.2
  56.8 0.0 all-gather.16.cloned.1.call-start
  56.9 47.0 %all_gather.27 = bf16[1536,192]{1,0:T(8,128)(2,1)S(1)} all-gather(bf16[192,192]{1,0:T(8,128)(2,1)} %param.11), channel_id=1, replica_groups=mesh['ctx'=64,'pair'=8] {'pair'}, dimensions={0}, use_global_device_ids=true | all-gather | bytes 663552 | tf_op jit(solution)/shard_map/all_gather | solution.py:37
  103.8 1.0 convolution_convert_fusion.1
  104.9 0.0 all-gather.10.cloned.1.call-start
  104.9 0.5 all-gather.10.cloned.1.call-update
  105.5 0.0 all-gather.12.cloned.1.call-start
  105.5 1.8 fusion.22
  107.3 92.1 %all-gather.14.cloned.1.call-done = bf16[8192,128]{1,0:T(8,128)(2,1)} async-done(((bf16[128,128]{1,0:T(8,128)(2,1)}), bf16[8192,128]{1,0:T(8,128)(2,1)}) %all-gather.14.cloned.1.call-update) | async-done | bytes 2097168 | tf_op jit(solution)/shard_map/all_gather | solution.py:48
  199.4 9.7 bitcast_reduce_fusion
  209.1 8.5 fusion.1
  217.6 107.9 %all-gather.16.cloned.1.call-done = bf16[8192,192]{0,1:T(8,128)(2,1)} async-done(((bf16[128,192]{0,1:T(8,128)(2,1)}), bf16[8192,192]{0,1:T(8,128)(2,1)}) %all-gather.16.cloned.1.call-update) | async-done | bytes 3145744 | tf_op jit(solution)/shard_map/all_gather | solution.py:49
  325.6 9.7 fusion.29
  335.3 50.5 %all-gather.10.cloned.1.call-done = bf16[768,1536]{1,0:T(8,128)(2,1)} async-done(((bf16[96,1536]{1,0:T(8,128)(2,1)}), bf16[768,1536]{1,0:T(8,128)(2,1)}) %all-gather.10.cloned.1.call-update) | async-done | bytes 2359312 | tf_op jit(solution)/shard_map/all_gather | solution.py:70
  385.8 2.9 fusion.66
  388.7 0.1 reduce_sum.28
  388.8 0.1 multiply_reduce_fusion
  389.0 0.2 fusion.23
  389.2 0.6 fusion.65
  389.9 37.2 %all_gather.30 = bf16[8,8,128]{2,1,0:T(8,128)(2,1)S(1)} all-gather(bf16[1,8,128]{2,1,0:T(8,128)(2,1)S(1)} %get-tuple-element.16), channel_id=1, replica_groups=mesh['ctx'=64,'pair'=8] {'pair'}, dimensions={0}, use_global_device_ids=true | all-gather | bytes 18432 | tf_op jit(solution)/shard_map/all_gather | solution.py:87
  427.1 1031.3 %all-gather.12.cloned.1.call-done = bf16[1,4096,128]{2,1,0:T(8,128)(2,1)} async-done(((bf16[1,8,128]{2,1,0:T(8,128)(2,1)}), bf16[1,4096,128]{2,1,0:T(8,128)(2,1)}) %all-gather.12.cloned.1.call-update) | async-done | bytes 1048592 | tf_op jit(solution)/shard_map/all_gather | solution.py:92
  1458.4 1.4 copy.30
  1459.9 0.3 multiply_convert_fusion
  1460.2 1.9 collective-permute-start
  1462.1 2.4 collective-permute-start.1
  1464.6 0.9 collective-permute-done
  1465.4 4.4 collective-permute-done.1
  1469.8 0.1 pad_maximum_fusion.5
  1469.9 4.0 collective-permute-start.2
  1473.9 1.5 collective-permute-start.3
  1475.4 0.2 pad_maximum_fusion.1
  1475.6 0.4 fusion.47
  1476.0 2.8 collective-permute-done.3
  1478.7 1.0 maximum_maximum_fusion
  1479.7 1.4 fusion.62
  1481.1 0.4 fusion.39
  1481.5 0.4 convolution_add_fusion.6
  1481.9 0.4 convolution_add_fusion.5
  1482.3 0.4 convolution_add_fusion.4
  1482.8 0.4 convolution_add_fusion.3
  1483.2 0.4 convolution_add_fusion.2
  1483.6 0.4 convolution_add_fusion.1
  1484.1 0.4 fusion.8
  1484.5 1.8 fusion.19
  (20 shorter events, 0.2 us)
Async XLA Ops:
  7.2 381.8 %copy-start = (bf16[1536,256]{1,0:T(8,128)(2,1)S(1)}, bf16[1536,256]{1,0:T(8,128)(2,1)}, u32[]{:S(2)}) copy-start(bf16[1536,256]{1,0:T(8,128)(2,1)} %param.14) | copy-start | bytes 2359300
  7.2 96.6 %copy-start.2 = (bf16[1,128,1536]{2,1,0:T(8,128)(2,1)S(1)}, bf16[1,128,1536]{2,1,0:T(8,128)(2,1)}, u32[]{:S(2)}) copy-start(bf16[1,128,1536]{2,1,0:T(8,128)(2,1)} %param.8) | copy-start | bytes 1179652
  7.2 98.3 %all-gather.8.cloned.1.call-start = ((), (), s32[]{:S(2)}) async-start(), calls=%async_computation | async-start | bytes 1769472 | tf_op jit(solution)/shard_map/all_gather | solution.py:35
  7.9 191.5 %all-gather.14.cloned.1.call-start = ((), (), s32[]{:S(2)}) async-start(), calls=%async_computation.3 | async-start | bytes 2129920 | tf_op jit(solution)/shard_map/all_gather | solution.py:48
  56.8 268.8 %all-gather.16.cloned.1.call-start = ((), (), s32[]{:S(2)}) async-start(), calls=%async_computation.4 | async-start | bytes 3194880 | tf_op jit(solution)/shard_map/all_gather | solution.py:49
  104.9 280.9 %all-gather.10.cloned.1.call-start = ((), (), s32[]{:S(2)}) async-start(), calls=%async_computation.1 | async-start | bytes 2654208 | tf_op jit(solution)/shard_map/all_gather | solution.py:70
  105.5 1352.9 %all-gather.12.cloned.1.call-start = ((), (), s32[]{:S(2)}) async-start(), calls=%async_computation.2 | async-start | bytes 1050624 | tf_op jit(solution)/shard_map/all_gather | solution.py:92
  385.8 3.2 copy-start.4
  1460.2 5.2 collective-permute-start
  1462.1 7.7 collective-permute-start.1
  1469.9 5.6 copy-start.3
  1469.9 6.0 collective-permute-start.2
  1473.9 4.8 collective-permute-start.3
  1484.1 2.3 copy-start.1
Sparse Core Ops, SparseCore 0:
  10.1 70.8 all-gather.7
  86.0 113.3 all-gather.13
  204.2 121.3 all-gather.15
  327.5 58.2 all-gather.9
  390.0 1068.3 all-gather.11
where the time goes:
time: 1520 us; the launch traced here: 1490 us
  waiting for transfers between devices  1290 us (85%)
  blocking collectives  131 us (9%)
  matrix products  31 us (2%)
    all_gather x1, waiting for transfers between devices, on_device(): gathered = lax.all_gather(colpart, ('ctx', 'pair'), axis=1, tiled=True)  1030 us
    all_gather x1, waiting for transfers between devices, on_device(): value_piece = lax.all_gather(values, 'ctx', axis=1, tiled=True)  108 us
    all_gather x1, waiting for transfers between devices, on_device(): key_piece = lax.all_gather(keys, 'ctx', axis=1, tiled=True)  92.1 us
    all_gather x1, waiting for transfers between devices, on_device(): lax.all_gather(w_out, 'pair', axis=0, tiled=True)  50.5 us
    all_gather x1, blocking collectives, on_device(): lax.all_gather(w_value, 'pair', axis=0, tiled=True)  47 us
    all_gather x1, blocking collectives, on_device(): lax.all_gather(w_key, 'pair', axis=0, tiled=True)  46.9 us
    all_gather x1, blocking collectives, on_device(): rows_all = lax.all_gather(rowpart, 'pair', axis=0, tiled=True)  37.2 us
  transfers between devices with their start and end apart: 9, of which 7 were waited for; matrix products, arithmetic and copies ran while one was open for 2% of the time, Pallas kernels for 0%

commit v1 on v0

v1 whole, which is shorter than its diff:
```python
import functools

import jax
import jax.numpy as jnp
from jax import lax
from jax.experimental import pallas as pl
from jax.experimental.pallas import tpu as pltpu
from jax.sharding import PartitionSpec as P

H = 4
KEY = 128
VAL = 192
PC = 128
POOL = 16
MESH = pl.DeviceIdType.MESH
BF = jnp.bfloat16
F32 = jnp.float32
BR = 384
HB = BR // 2
VMEM_LIMIT = 60 * 1024 * 1024


def coords():
    c = lax.axis_index("ctx")
    p = lax.axis_index("pair")
    return c, p, c // 32, (c // 8) % 4, (c // 2) % 4, c % 2


def ctx_of(zh, x, y, core):
    return ((zh * 4 + x) * 4 + y) * 2 + core


def at_z(c, zh, p, d):
    z = (zh * 8 + p + d + 16) % 16
    return ((z // 8) * 32 + c % 32, z % 8)


def rcopy(src, dst, ssem, rsem, dev):
    return pltpu.make_async_remote_copy(
        src_ref=src, dst_ref=dst, send_sem=ssem, recv_sem=rsem, device_id=dev, device_id_type=MESH
    )


def enter(devs):
    barrier = pltpu.get_barrier_semaphore()
    for dev in devs:
        pl.semaphore_signal(barrier, inc=1, device_id=dev, device_id_type=MESH)
    pl.semaphore_wait(barrier, len(devs))


def weights_kernel(wk, wv, wq, wo, WK, WV, WQ, WO, ss, rs, ps, pr, ls):
    c, p, zh, x, y, h = coords()
    partner = (c + 1 - 2 * h, p)
    dirs = (1, -1)
    nxt = [at_z(c, zh, p, d) for d in dirs]
    enter(nxt + [partner])
    arrs = ((wk, WK), (wv, WV), (wq, WQ), (wo, WO))
    locs = []
    for i, (src, out) in enumerate(arrs):
        r = src.shape[0]
        cp = pltpu.make_async_copy(src, out.at[pl.ds(pl.multiple_of(p * r, r), r), :], ls.at[i])
        cp.start()
        locs.append(cp)

    def part(i, shard, lanes=None):
        src, out = arrs[i]
        r = src.shape[0]
        hr = r // 2
        row = pl.ds(pl.multiple_of(shard * r + h * hr, hr), hr)
        return out.at[row, :] if lanes is None else out.at[row, lanes]

    def last(di):
        if di == 0:
            return ((0, None), (2, pl.ds(0, 256)), (3, pl.ds(0, 768)))
        return ((1, None), (2, pl.ds(256, 256)), (3, pl.ds(768, 768)))

    sent = []
    for group in ((0, 1, 2), (3,)):
        for di, d in enumerate(dirs):
            for i in group:
                src, _ = arrs[i]
                hr = src.shape[0] // 2
                cp = rcopy(
                    src.at[pl.ds(pl.multiple_of(h * hr, hr), hr), :],
                    part(i, p),
                    ss.at[di, 0, i],
                    rs.at[di, 0, i],
                    nxt[di],
                )
                cp.start()
                sent.append(cp)
        for t in (1, 2, 3):
            for di, d in enumerate(dirs):
                shard = (p - d * t + 8) % 8
                for i in group:
                    here = part(i, shard)
                    rcopy(here, here, ss.at[di, t - 1, i], rs.at[di, t - 1, i], nxt[di]).wait_recv()
                    if t < 3:
                        cp = rcopy(here, here, ss.at[di, t, i], rs.at[di, t, i], nxt[di])
                        cp.start()
                        sent.append(cp)
                    else:
                        for j, lanes in last(di):
                            if j == i:
                                ref = part(i, shard, lanes)
                                cp = rcopy(ref, ref, ss.at[di, 3, i], rs.at[di, 3, i], nxt[di])
                                cp.start()
                                sent.append(cp)
                    k = (t - 1) * 2 + di
                    cp = rcopy(here, here, ps.at[k, i], pr.at[k, i], partner)
                    cp.start()
                    sent.append(cp)
        shard = (p + 4) % 8
        for i in group:
            for di in range(2):
                for j, lanes in last(di):
                    if j == i:
                        ref = part(i, shard, lanes)
                        rcopy(ref, ref, ss.at[di, 3, i], rs.at[di, 3, i], nxt[di]).wait_recv()
            here = part(i, shard)
            cp = rcopy(here, here, ps.at[6, i], pr.at[6, i], partner)
            cp.start()
            sent.append(cp)
    g = 1 - h
    for i, (src, out) in enumerate(arrs):
        r = src.shape[0]
        hr = r // 2
        for k in range(7):
            if k < 6:
                shard = (p - dirs[k % 2] * (k // 2 + 1) + 8) % 8
            else:
                shard = (p + 4) % 8
            ref = out.at[pl.ds(pl.multiple_of(shard * r + g * hr, hr), hr), :]
            rcopy(ref, ref, ps.at[k, i], pr.at[k, i], partner).wait_recv()
    for cp in sent:
        cp.wait_send()
    for cp in locs:
        cp.wait()


def gather_weights(wk, wv, wq, wo):
    anyspec = pl.BlockSpec(memory_space=pltpu.VMEM)
    outs = tuple(jax.ShapeDtypeStruct((8 * w.shape[0], w.shape[1]), BF) for w in (wk, wv, wq, wo))
    dma = pltpu.SemaphoreType.DMA
    return pl.pallas_call(
        weights_kernel,
        out_shape=outs,
        in_specs=[anyspec] * 4,
        out_specs=(anyspec,) * 4,
        scratch_shapes=[dma((2, 4, 4)), dma((2, 4, 4)), dma((7, 4)), dma((7, 4)), dma((4,))],
        compiler_params=pltpu.CompilerParams(
            collective_id=0, has_side_effects=True, vmem_limit_bytes=VMEM_LIMIT
        ),
        name="weights",
    )(wk, wv, wq, wo)


def project_kernel(tok, WK, WV, WQ, kv, q):
    t = tok[...]
    kv[0:128, :] = jnp.dot(t, WK[...], preferred_element_type=F32).astype(BF)
    v = jnp.dot(t, WV[...], preferred_element_type=F32)
    kv[128:256, :] = v[:, :128].astype(BF)
    lane = lax.broadcasted_iota(jnp.int32, (128, 64), 1)
    ones = jnp.where(lane == 0, 1.0, 0.0).astype(F32)
    kv[256:384, :] = jnp.concatenate([v[:, 128:192], ones], axis=1).astype(BF)
    qq = jnp.dot(t, WQ[...], preferred_element_type=F32).astype(BF)
    for h in range(H):
        q[h * 128 : (h + 1) * 128, :] = qq[:, h * KEY : (h + 1) * KEY]


def project(tok, WK, WV, WQ):
    vm = pl.BlockSpec(memory_space=pltpu.VMEM)
    return pl.pallas_call(
        project_kernel,
        out_shape=(jax.ShapeDtypeStruct((BR, 128), BF), jax.ShapeDtypeStruct((512, 128), BF)),
        in_specs=[vm] * 4,
        out_specs=(vm, vm),
        compiler_params=pltpu.CompilerParams(vmem_limit_bytes=VMEM_LIMIT),
        name="project",
    )(tok, WK, WV, WQ)


def kv_kernel(blk, OUT, relay, ss, rs, ps, pr, zs, zr, ls):
    c, p, zh, x, y, h = coords()
    partner = (c + 1 - 2 * h, p)

    def slot(g, da, db, core=None):
        core = h if core is None else core
        z = zh if g == 0 else 1 - zh
        xx = (x + da * (1 - core) + db * core + 8) % 4
        yy = (y + da * core + db * (1 - core) + 8) % 4
        return ctx_of(z, xx, yy, core)

    ap, am = (slot(0, 1, 0), p), (slot(0, -1, 0), p)
    bp, bm = (slot(0, 0, 1), p), (slot(0, 0, -1), p)
    zp, zm = at_z(c, zh, p, 4), at_z(c, zh, p, -4)
    enter([ap, am, bp, bm, zp, zm, partner])
    sent = []

    def start(src, dst, s, r, dev):
        cp = rcopy(src, dst, s, r, dev)
        cp.start()
        sent.append(cp)

    loc = pltpu.make_async_copy(blk, OUT.at[c], ls.at[0])
    loc.start()
    top, bot = pl.ds(0, HB), pl.ds(HB, HB)
    halves = (top, bot)
    DA = (0, -1, 1, 2)

    def whole(g, s, own):
        return blk if own else OUT.at[s]

    def half(s, k):
        return OUT.at[s, halves[k], :]

    def to_a(g, own):
        s = slot(g, 0, 0)
        src = whole(g, s, own)
        start(src, OUT.at[s], ss.at[20 * g], rs.at[20 * g], ap)
        start(src, OUT.at[s], ss.at[20 * g + 1], rs.at[20 * g + 1], am)

    def to_b(g, j, own=False):
        s = slot(g, DA[j], 0)
        src = whole(g, s, own)
        k = 20 * g + 4 + 4 * j
        start(src, OUT.at[s], ss.at[k], rs.at[k], bp)
        start(src, OUT.at[s], ss.at[k + 1], rs.at[k + 1], bm)

    def to_partner(g, j, m, own=False):
        s = slot(g, DA[j], DA[m])
        k = 16 * g + 4 * j + m
        start(whole(g, s, own), OUT.at[s], ps.at[k], pr.at[k], partner)

    def got(ref, k):
        rcopy(ref, ref, ss.at[k], rs.at[k], partner).wait_recv()

    def a_near(g):
        for j, k, dev, hf in ((1, 0, ap, 0), (2, 1, am, 1)):
            s = slot(g, DA[j], 0)
            got(OUT.at[s], 20 * g + k)
            start(half(s, hf), half(s, hf), ss.at[20 * g + 2 + hf], rs.at[20 * g + 2 + hf], dev)
            to_b(g, j)
            to_partner(g, j, 0)

    def a_far(g):
        s = slot(g, 2, 0)
        got(half(s, 0), 20 * g + 2)
        got(half(s, 1), 20 * g + 3)
        to_b(g, 3)
        to_partner(g, 3, 0)

    def b_near(g, j):
        base = 20 * g + 4 + 4 * j
        for m, k, dev, hf in ((1, 0, bp, 0), (2, 1, bm, 1)):
            s = slot(g, DA[j], DA[m])
            got(OUT.at[s], base + k)
            start(half(s, hf), half(s, hf), ss.at[base + 2 + hf], rs.at[base + 2 + hf], dev)
            to_partner(g, j, m)

    def b_far(g, j):
        base = 20 * g + 4 + 4 * j
        s = slot(g, DA[j], 2)
        got(half(s, 0), base + 2)
        got(half(s, 1), base + 3)
        to_partner(g, j, 3)

    to_a(0, True)
    start(blk.at[top, :], relay.at[0], zs.at[0], zr.at[0], zp)
    start(blk.at[bot, :], relay.at[1], zs.at[1], zr.at[1], zm)
    to_b(0, 0, True)
    to_partner(0, 0, 0, True)
    a_near(0)
    b_near(0, 0)
    a_far(0)
    o1 = at_z(c, zh, p, -4)[0]
    o2 = at_z(c, zh, p, 4)[0]
    rcopy(relay.at[0], relay.at[0], zs.at[0], zr.at[0], zp).wait_recv()
    start(relay.at[0], OUT.at[o1, top, :], zs.at[2], zr.at[2], zp)
    rcopy(relay.at[1], relay.at[1], zs.at[1], zr.at[1], zm).wait_recv()
    start(relay.at[1], OUT.at[o2, bot, :], zs.at[3], zr.at[3], zm)
    b_far(0, 0)
    b_near(0, 1)
    b_near(0, 2)
    other = slot(1, 0, 0)
    r0, r1 = half(other, 0), half(other, 1)
    rcopy(r0, r0, zs.at[2], zr.at[2], zp).wait_recv()
    rcopy(r1, r1, zs.at[3], zr.at[3], zm).wait_recv()
    to_a(1, False)
    to_b(1, 0)
    to_partner(1, 0, 0)
    b_near(0, 3)
    b_far(0, 1)
    b_far(0, 2)
    b_far(0, 3)
    a_near(1)
    b_near(1, 0)
    a_far(1)
    b_far(1, 0)
    for j in (1, 2, 3):
        b_near(1, j)
    for j in (1, 2, 3):
        b_far(1, j)
    for g in range(2):
        for j in range(4):
            for m in range(4):
                s = slot(g, DA[j], DA[m], 1 - h)
                k = 16 * g + 4 * j + m
                rcopy(OUT.at[s], OUT.at[s], ps.at[k], pr.at[k], partner).wait_recv()
    for cp in sent:
        cp.wait_send()
    loc.wait()


def gather_kv(blk):
    vm = pl.BlockSpec(memory_space=pltpu.VMEM)
    dma = pltpu.SemaphoreType.DMA
    return pl.pallas_call(
        kv_kernel,
        out_shape=jax.ShapeDtypeStruct((64, BR, 128), BF),
        in_specs=[vm],
        out_specs=vm,
        scratch_shapes=[
            pltpu.VMEM((2, HB, 128), BF),
            dma((40,)),
            dma((40,)),
            dma((32,)),
            dma((32,)),
            dma((4,)),
            dma((4,)),
            dma((1,)),
        ],
        compiler_params=pltpu.CompilerParams(
            collective_id=1, has_side_effects=True, vmem_limit_bytes=VMEM_LIMIT
        ),
        name="gather_kv",
    )(blk)


CHUNK = 8


def attend_kernel(q_ref, kv_ref, tok, WO, gain, wpair, seq, rows, cols, acc, mixed):
    scale = KEY ** (-0.5) * 1.4426950408889634

    def step(i, m):
        blk = kv_ref[pl.ds(i * CHUNK, CHUNK)]
        n = CHUNK * 128
        k = blk[:, 0:128, :].reshape(n, 128)
        v1 = blk[:, 128:256, :].reshape(n, 128)
        v2 = blk[:, 256:384, :].reshape(n, 128)
        v = jnp.concatenate([v1, v2], axis=1)
        s = lax.dot_general(q_ref[...], k, (((1,), (1,)), ((), ())), preferred_element_type=F32)
        s = s * scale
        m2 = jnp.maximum(m, jnp.max(s, axis=1, keepdims=True))
        w = jnp.exp2(s - m2).astype(BF)
        o = jnp.dot(w, v, preferred_element_type=F32)
        acc[...] = acc[...] * jnp.exp2(m - m2) + o
        return m2

    acc[...] = jnp.zeros_like(acc)
    lax.fori_loop(0, 64 // CHUNK, step, jnp.full((512, 1), -1e30, F32))
    a = acc[...]
    mx = (a[:, 0:VAL] / a[:, VAL : VAL + 1]).astype(BF)
    for h in range(H):
        mixed[:, h * VAL : (h + 1) * VAL] = mx[h * 128 : (h + 1) * 128, :]
    summed = tok[...].astype(F32) + jnp.dot(mixed[...], WO[...], preferred_element_type=F32)
    seq[...] = summed.astype(BF)
    pooled = jnp.mean(summed.reshape(8, POOL, summed.shape[1]), axis=1)
    ms = jnp.mean(pooled * pooled, axis=-1, keepdims=True)
    normed = (pooled * lax.rsqrt(ms + 1e-06) * gain[...]).astype(BF)
    both = jnp.dot(normed, wpair[...], preferred_element_type=F32).astype(BF)
    rows[...] = both[:, :PC]
    cols[...] = both[:, PC:]


def attend(q, kv, tok, WO, gain, wpair):
    vm = pl.BlockSpec(memory_space=pltpu.VMEM)
    return pl.pallas_call(
        attend_kernel,
        out_shape=(
            jax.ShapeDtypeStruct(tok.shape, BF),
            jax.ShapeDtypeStruct((8, PC), BF),
            jax.ShapeDtypeStruct((8, PC), BF),
        ),
        in_specs=[vm] * 6,
        out_specs=(vm,) * 3,
        scratch_shapes=[pltpu.VMEM((512, 256), F32), pltpu.VMEM((128, H * VAL), BF)],
        compiler_params=pltpu.CompilerParams(vmem_limit_bytes=VMEM_LIMIT),
        name="attend",
    )(q, kv, tok, WO, gain, wpair)


def pair_kernel(rb, cb, RB, CB, HM, HL, HR, rs_s, rs_r, z_s, z_r, x_s, x_r, y_s, y_r, ls):
    c, p, zh, x, y, h = coords()
    flip = c + 32 - 64 * zh
    cn, cv = (c + 1) % 64, (c + 63) % 64
    pp = [(p + k) % 8 for k in range(8)]
    devs = [(c, pp[k]) for k in range(1, 8)] + [(flip, q) for q in range(8)]
    devs += [(cn, q) for q in range(8)] + [(cv, q) for q in range(8)]
    xs = [(ctx_of(zh, (x + k) % 4, y, h), p) for k in (1, 2, 3)]
    yc = []
    for k in range(4):
        for e in range(2):
            if k or e:
                yc.append((ctx_of(zh, x, (y + k) % 4, (h + e) % 2), p))
    enter(devs + xs + yc)

    def local(src, dst, k):
        cp = pltpu.make_async_copy(src, dst, ls.at[k])
        cp.start()
        cp.wait()

    tgt = c // 8
    jobs = [(tgt, HM, 0, None), (tgt + 1, HL, 1, (c % 8 == 7) & (tgt < 7)), (tgt - 1, HR, 2, (c % 8 == 0) & (tgt > 0))]

    def cond(pred, fn):
        if pred is None:
            fn()
        else:
            pl.when(pred)(fn)

    def col_sends(wait):
        for t, buf, b, pred in jobs:
            for f in range(2):
                dc = c if f == 0 else flip

                def go(t=t, buf=buf, b=b, f=f, dc=dc):
                    cp = rcopy(cb, buf.at[p], z_s.at[b, f], z_r.at[b, p], (dc, t))
                    cp.wait_send() if wait else cp.start()

                if f == 1:
                    cond(pred, go)
                else:
                    away = t != p
                    cond(away if pred is None else away & pred, go)

    col_sends(False)
    for t, buf, b, pred in jobs:
        mine = (t == p) if pred is None else (t == p) & pred
        pl.when(mine)(functools.partial(local, cb, buf.at[p], b))

    def row_sends(wait):
        for k in range(1, 8):
            cp = rcopy(rb, RB.at[1, p], rs_s.at[1, k], rs_r.at[1, p], (c, pp[k]))
            cp.wait_send() if wait else cp.start()
        for b, dc, pred in ((0, cn, c < 63), (2, cv, c > 0)):

            @pl.when(pred)
            def _():
                for k in range(8):
                    cp = rcopy(rb, RB.at[b, p], rs_s.at[b, k], rs_r.at[b, p], (dc, pp[k]))
                    cp.wait_send() if wait else cp.start()

    row_sends(False)
    local(rb, RB.at[1, p], 3)

    @pl.when(c == 0)
    def _():
        RB[0] = jnp.zeros((8, 8, PC), BF)

    @pl.when(c == 63)
    def _():
        RB[2] = jnp.zeros((8, 8, PC), BF)

    @pl.when(p == 0)
    def _():
        CB[0] = jnp.zeros((8, 8, PC), BF)

    @pl.when(p == 7)
    def _():
        CB[9] = jnp.zeros((8, 8, PC), BF)

    def spread(buf, b, owner, member, cslot):
        ox = owner % 4
        oz = owner // 4
        holder = member & (x == ox)

        @pl.when(holder)
        def _():
            for s in range(8):

                @pl.when((s != p) | (zh != oz))
                def _():
                    rcopy(buf.at[s], buf.at[s], z_s.at[b, 0], z_r.at[b, s], (c, p)).wait_recv()

            for k in range(3):
                rcopy(buf, buf, x_s.at[b, k], x_r.at[b], xs[k]).start()

        @pl.when(member & (x != ox))
        def _():
            rcopy(buf, buf, x_s.at[b, 0], x_r.at[b], (c, p)).wait_recv()

        @pl.when(member)
        def _():
            for k in range(7):
                rcopy(buf, CB.at[cslot], y_s.at[b, k], y_r.at[cslot], yc[k]).start()
            local(buf, CB.at[cslot], 4 + b)
            for k in range(7):
                rcopy(buf, CB.at[cslot], y_s.at[b, k], y_r.at[cslot], yc[k]).wait_send()

        @pl.when(holder)
        def _():
            for k in range(3):
                rcopy(buf, buf, x_s.at[b, k], x_r.at[b], xs[k]).wait_send()

    always = c >= 0
    mine = 1 + 2 * y + h
    lmem = (y == 3) & (h == 1) & (p > 0)
    rmem = (y == 0) & (h == 0) & (p < 7)
    spread(HM, 0, p, always, mine)
    spread(HL, 1, p - 1, lmem, 0)
    spread(HR, 2, p + 1, rmem, 9)

    for k in range(8):

        @pl.when(mine != k + 1)
        def _():
            rcopy(CB.at[k + 1], CB.at[k + 1], y_s.at[0, 0], y_r.at[k + 1], (c, p)).wait_recv()

    @pl.when((p > 0) & jnp.logical_not((y == 3) & (h == 1)))
    def _():
        rcopy(CB.at[0], CB.at[0], y_s.at[0, 0], y_r.at[0], (c, p)).wait_recv()

    @pl.when((p < 7) & jnp.logical_not((y == 0) & (h == 0)))
    def _():
        rcopy(CB.at[9], CB.at[9], y_s.at[0, 0], y_r.at[9], (c, p)).wait_recv()

    for k in range(1, 8):
        rcopy(RB.at[1, pp[k]], RB.at[1, pp[k]], rs_s.at[1, 1], rs_r.at[1, pp[k]], (c, p)).wait_recv()
    for b, pred in ((0, c > 0), (2, c < 63)):

        @pl.when(pred)
        def _():
            for k in range(8):
                rcopy(RB.at[b, k], RB.at[b, k], rs_s.at[b, 0], rs_r.at[b, k], (c, p)).wait_recv()

    row_sends(True)
    col_sends(True)


def exchange(rb, cb):
    vm = pl.BlockSpec(memory_space=pltpu.VMEM)
    dma = pltpu.SemaphoreType.DMA
    hold = pltpu.VMEM((8, 8, PC), BF)
    return pl.pallas_call(
        pair_kernel,
        out_shape=(jax.ShapeDtypeStruct((3, 8, 8, PC), BF), jax.ShapeDtypeStruct((10, 8, 8, PC), BF)),
        in_specs=[vm] * 2,
        out_specs=(vm,) * 2,
        scratch_shapes=[
            hold,
            hold,
            hold,
            dma((3, 8)),
            dma((3, 8)),
            dma((3, 2)),
            dma((3, 8)),
            dma((3, 3)),
            dma((3,)),
            dma((3, 7)),
            dma((10,)),
            dma((7,)),
        ],
        compiler_params=pltpu.CompilerParams(
            collective_id=2, has_side_effects=True, vmem_limit_bytes=VMEM_LIMIT
        ),
        name="exchange",
    )(rb, cb)


def conv_kernel(rb, cb, w, out):
    def seq(s, carry):
        prev = rb[0, pl.ds(s, 1)].reshape(8, PC).astype(F32)
        own = rb[1, pl.ds(s, 1)].reshape(8, PC).astype(F32)
        nxt = rb[2, pl.ds(s, 1)].reshape(8, PC).astype(F32)
        col = jnp.concatenate([cb[k, pl.ds(s, 1)].reshape(8, PC) for k in range(10)], axis=0).astype(F32)
        rows = [prev[6:7], prev[7:8]] + [own[k : k + 1] for k in range(8)] + [nxt[0:1], nxt[1:2]]
        shifted = [col[6 + 2 * b : 70 + 2 * b] for b in range(3)]
        maps = [[(r * cs).astype(BF) for r in rows] for cs in shifted]
        for i in range(8):
            lhs = jnp.concatenate(
                [maps[b][i + 2 * a] for a in range(3) for b in range(3)], axis=1
            )
            t = jnp.dot(lhs, w[...], preferred_element_type=F32)
            res = maps[1][i + 2].astype(F32) + jax.nn.gelu(t)
            out[pl.ds(s, 1), i] = res.astype(BF).reshape(1, 64, PC)
        return carry

    lax.fori_loop(0, 8, seq, 0)


def convolve(rb, cb, w):
    vm = pl.BlockSpec(memory_space=pltpu.VMEM)
    return pl.pallas_call(
        conv_kernel,
        out_shape=jax.ShapeDtypeStruct((8, 8, 64, PC), BF),
        in_specs=[vm] * 3,
        out_specs=vm,
        compiler_params=pltpu.CompilerParams(vmem_limit_bytes=VMEM_LIMIT),
        name="convolve",
    )(rb, cb, w)


def on_device(tokens, w_query, w_key, w_value, w_out, norm_gain, w_pair, conv_weight):
    tok = tokens.reshape(tokens.shape[1], tokens.shape[2])
    WK, WV, WQ, WO = gather_weights(w_key, w_value, w_query, w_out)
    blk, q = project(tok, WK, WV, WQ)
    kv = gather_kv(blk)
    seq, rows, cols = attend(q, kv, tok, WO, norm_gain.reshape(1, -1), w_pair)
    rb, cb = exchange(rows, cols)
    out = convolve(rb, cb, conv_weight.reshape(9 * PC, PC))
    return seq.reshape(tokens.shape), out


def solution(mesh):
    return jax.shard_map(
        on_device,
        mesh=mesh,
        in_specs=(
            P("pair", "ctx", None),
            P("pair", None),
            P("pair", None),
            P("pair", None),
            P("pair", None),
            P(),
            P(),
            P(),
        ),
        out_specs=(P("pair", "ctx", None), P(None, "ctx", "pair", None)),
        check_vma=False,
    )
```

time: 1520 us -> 156 us (0.10); the launches traced: 1490 us -> 155 us
  waiting for transfers between devices: 1290 us -> 0 us
  Pallas kernels: 0 us -> 153 us
  blocking collectives: 131 us -> 0 us
  matrix products: 31 us -> 0 us
    all_gather x5 -> x0, waiting for transfers between devices: 1280 us -> none  [the longest x1 1030 us: on_device(): gathered = lax.all_gather(colpart, ('ctx', 'pair'), axis=1, tiled=True)]
    pallas_call x0 -> x6, Pallas kernels: none -> 153 us  [the longest x1 54.9 us: gather_weights(): pl.pallas_call(weights_kernel, out_shape=outs, in_specs=[anyspec] * 4, ou...]
    all_gather x3 -> x0, blocking collectives: 131 us -> none  [the longest x1 47 us: on_device(): lax.all_gather(w_value, 'pair', axis=0, tiled=True)]
    dot_general x16 -> x0, matrix products: 31 us -> none  [the longest x1 9.71 us: on_device(): jnp.einsum('bhqn,bnv->bhqv', weights.astype(jnp.bfloat16), value_piece, p...]
  transfers between devices with their start and end apart: 9 -> 0, of which waited for: 7 -> 0; matrix products, arithmetic and copies ran while one was open for 2% -> 0% of each run, Pallas kernels for 0% -> 0%
where the time goes in v1:
time: 156 us; the launch traced here: 155 us
  Pallas kernels  153 us (98%)
    pallas_call x1, Pallas kernels, gather_weights(): pl.pallas_call(weights_kernel, out_shape=outs, in_specs=[anyspec] * 4, ou...  54.9 us
    pallas_call x1, Pallas kernels, gather_kv(): pl.pallas_call(kv_kernel, out_shape=jax.ShapeDtypeStruct((64, BR, 128), B...  43.7 us
    pallas_call x1, Pallas kernels, exchange(): pl.pallas_call(pair_kernel, out_shape=(jax.ShapeDtypeStruct((3, 8, 8, PC)...  28.7 us
    pallas_call x1, Pallas kernels, attend(): pl.pallas_call(attend_kernel, out_shape=(jax.ShapeDtypeStruct(tok.shape,...  16.3 us
    pallas_call x1, Pallas kernels, convolve(): pl.pallas_call(conv_kernel, out_shape=jax.ShapeDtypeStruct((8, 8, 64, PC)...  6.14 us
    pallas_call x1, Pallas kernels, project(): pl.pallas_call(project_kernel, out_shape=(jax.ShapeDtypeStruct((BR, 128),...  3.12 us

profile of v1, /device:TPU:1, one launch (start us, length us, event | category | flops | bytes accessed | tf_op | source)
XLA Modules:
  0.0 154.8 jit_solution(3270086392170717847)
XLA Ops:
  0.6 1.3 reshape.17.gain
  1.9 54.9 %weights.1 = (bf16[1536,128]{1,0:T(8,128)(2,1)}, bf16[1536,192]{1,0:T(8,128)(2,1)}, bf16[1536,512]{1,0:T(8,128)(2,1)}, bf16[768,1536]{1,0:T(8,128)(2,1)}) custom-call(bf16[192,128]{1,0:T(8,128)(2,1)} %wk.1, bf16[192,192]{1,0:T(8,128)(2,1)} %wv.1, bf16[192,512]{1,0:T(8,128)(2,1)} %wq.1, bf16[96,1536]{1,0:T(8,128)(2,1)} %wo.1), custom_call_target="tpu_custom_call" | custom-call | tf_op jit(solution)/shard_map/weights/pallas_call | solution.py:145
  56.8 3.1 %project.1 = (bf16[384,128]{1,0:T(8,128)(2,1)}, bf16[512,128]{1,0:T(8,128)(2,1)}) custom-call(bf16[128,1536]{1,0:T(8,128)(2,1)} %bitcast.3, bf16[1536,128]{1,0:T(8,128)(2,1)} %get-tuple-element.13.WK, bf16[1536,192]{1,0:T(8,128)(2,1)} %get-tuple-element.14.WV, bf16[1536,512]{1,0:T(8,128)(2,1)} %get-tuple-element.15.WQ), custom_call_target="tpu_custom_call" | custom-call | tf_op jit(solution)/shard_map/project/pallas_call | solution.py:173
  59.9 43.7 %gather_kv.1.kv_ref = bf16[64,384,128]{2,1,0:T(8,128)(2,1)} custom-call(bf16[384,128]{1,0:T(8,128)(2,1)} %get-tuple-element.17.blk), custom_call_target="tpu_custom_call" | custom-call | tf_op jit(solution)/shard_map/gather_kv/pallas_call | solution.py:318
  103.7 16.3 %attend.1 = (bf16[128,1536]{1,0:T(8,128)(2,1)}, bf16[8,128]{1,0:T(8,128)(2,1)}, bf16[8,128]{1,0:T(8,128)(2,1)}) custom-call(bf16[512,128]{1,0:T(8,128)(2,1)} %get-tuple-element.16.q_ref, bf16[64,384,128]{2,1,0:T(8,128)(2,1)} %gather_kv.1.kv_ref, bf16[128,1536]{1,0:T(8,128)(2,1)} %bitcast.4, bf16[768,1536]{1,0:T(8,128)(2,1)} %get-tuple-element.18.WO, ...), custom_call_target="tpu_custom_call" | custom-call | tf_op jit(solution)/shard_map/attend/pallas_call | solution.py:379
  120.0 28.7 %exchange.1 = (bf16[3,8,8,128]{3,2,1,0:T(8,128)(2,1)}, bf16[10,8,8,128]{3,2,1,0:T(8,128)(2,1)}) custom-call(bf16[8,128]{1,0:T(8,128)(2,1)} %get-tuple-element.20.rb, bf16[8,128]{1,0:T(8,128)(2,1)} %get-tuple-element.21.cb), custom_call_target="tpu_custom_call" | custom-call | tf_op jit(solution)/shard_map/exchange/pallas_call | solution.py:546
  148.7 6.1 %convolve.1 = bf16[8,8,64,128]{3,2,1,0:T(8,128)(2,1)} custom-call(bf16[3,8,8,128]{3,2,1,0:T(8,128)(2,1)} %get-tuple-element.22.rb, bf16[10,8,8,128]{3,2,1,0:T(8,128)(2,1)} %get-tuple-element.23.cb, bf16[1152,128]{1,0:T(8,128)(2,1)} %bitcast.5), custom_call_target="tpu_custom_call" | custom-call | tf_op jit(solution)/shard_map/convolve/pallas_call | solution.py:595

commit v2 on v0

v2 whole, which is shorter than its diff:
```python
import functools

import jax
import jax.numpy as jnp
from jax import lax
from jax.experimental import pallas as pl
from jax.experimental.pallas import tpu as pltpu
from jax.sharding import PartitionSpec as P

H = 4
KEY = 128
VAL = 192
PC = 128
POOL = 16
MESH = pl.DeviceIdType.MESH
BF = jnp.bfloat16
F32 = jnp.float32
BR = 320
HB = BR // 2
VMEM_LIMIT = 60 * 1024 * 1024


def coords():
    c = lax.axis_index("ctx")
    p = lax.axis_index("pair")
    return c, p, c // 32, (c // 8) % 4, (c // 2) % 4, c % 2


def ctx_of(zh, x, y, core):
    return ((zh * 4 + x) * 4 + y) * 2 + core


def at_z(c, zh, p, d):
    z = (zh * 8 + p + d + 16) % 16
    return ((z // 8) * 32 + c % 32, z % 8)


def rcopy(src, dst, ssem, rsem, dev):
    return pltpu.make_async_remote_copy(
        src_ref=src, dst_ref=dst, send_sem=ssem, recv_sem=rsem, device_id=dev, device_id_type=MESH
    )


def enter(devs):
    barrier = pltpu.get_barrier_semaphore()
    for dev in devs:
        pl.semaphore_signal(barrier, inc=1, device_id=dev, device_id_type=MESH)
    pl.semaphore_wait(barrier, len(devs))


def exchange(rb, cb, RB, CB, HM, HL, HR, rs_s, rs_r, z_s, z_r, x_s, x_r, y_s, y_r, ls):
    c, p, zh, x, y, h = coords()
    flip = c + 32 - 64 * zh
    cn, cv = (c + 1) % 64, (c + 63) % 64
    pp = [(p + k) % 8 for k in range(8)]
    xs = [(ctx_of(zh, (x + k) % 4, y, h), p) for k in (1, 2, 3)]
    yc = []
    for k in range(4):
        for e in range(2):
            if k or e:
                yc.append((ctx_of(zh, x, (y + k) % 4, (h + e) % 2), p))

    def local(src, dst, k):
        cp = pltpu.make_async_copy(src, dst, ls.at[k])
        cp.start()
        cp.wait()

    tgt = c // 8
    jobs = [(tgt, HM, 0, None), (tgt + 1, HL, 1, (c % 8 == 7) & (tgt < 7)), (tgt - 1, HR, 2, (c % 8 == 0) & (tgt > 0))]

    def cond(pred, fn):
        if pred is None:
            fn()
        else:
            pl.when(pred)(fn)

    def col_sends(wait):
        for t, buf, b, pred in jobs:
            for f in range(2):
                dc = c if f == 0 else flip

                def go(t=t, buf=buf, b=b, f=f, dc=dc):
                    cp = rcopy(cb, buf.at[p], z_s.at[b, f], z_r.at[b, p], (dc, t))
                    cp.wait_send() if wait else cp.start()

                if f == 1:
                    cond(pred, go)
                else:
                    away = t != p
                    cond(away if pred is None else away & pred, go)

    col_sends(False)
    for t, buf, b, pred in jobs:
        mine = (t == p) if pred is None else (t == p) & pred
        pl.when(mine)(functools.partial(local, cb, buf.at[p], b))

    def row_sends(wait):
        for k in range(1, 8):
            cp = rcopy(rb, RB.at[1, p], rs_s.at[1, k], rs_r.at[1, p], (c, pp[k]))
            cp.wait_send() if wait else cp.start()
        for b, dc, pred in ((0, cn, c < 63), (2, cv, c > 0)):

            @pl.when(pred)
            def _():
                for k in range(8):
                    cp = rcopy(rb, RB.at[b, p], rs_s.at[b, k], rs_r.at[b, p], (dc, pp[k]))
                    cp.wait_send() if wait else cp.start()

    row_sends(False)
    local(rb, RB.at[1, p], 3)

    @pl.when(c == 0)
    def _():
        RB[0] = jnp.zeros((8, 8, PC), BF)

    @pl.when(c == 63)
    def _():
        RB[2] = jnp.zeros((8, 8, PC), BF)

    @pl.when(p == 0)
    def _():
        CB[0] = jnp.zeros((8, 8, PC), BF)

    @pl.when(p == 7)
    def _():
        CB[9] = jnp.zeros((8, 8, PC), BF)

    def spread(buf, b, owner, member, cslot):
        ox = owner % 4
        oz = owner // 4
        holder = member & (x == ox)

        @pl.when(holder)
        def _():
            for s in range(8):

                @pl.when((s != p) | (zh != oz))
                def _():
                    rcopy(buf.at[s], buf.at[s], z_s.at[b, 0], z_r.at[b, s], (c, p)).wait_recv()

            for k in range(3):
                rcopy(buf, buf, x_s.at[b, k], x_r.at[b], xs[k]).start()

        @pl.when(member & (x != ox))
        def _():
            rcopy(buf, buf, x_s.at[b, 0], x_r.at[b], (c, p)).wait_recv()

        @pl.when(member)
        def _():
            for k in range(7):
                rcopy(buf, CB.at[cslot], y_s.at[b, k], y_r.at[cslot], yc[k]).start()
            local(buf, CB.at[cslot], 4 + b)
            for k in range(7):
                rcopy(buf, CB.at[cslot], y_s.at[b, k], y_r.at[cslot], yc[k]).wait_send()

        @pl.when(holder)
        def _():
            for k in range(3):
                rcopy(buf, buf, x_s.at[b, k], x_r.at[b], xs[k]).wait_send()

    always = c >= 0
    mine = 1 + 2 * y + h
    lmem = (y == 3) & (h == 1) & (p > 0)
    rmem = (y == 0) & (h == 0) & (p < 7)
    spread(HM, 0, p, always, mine)
    spread(HL, 1, p - 1, lmem, 0)
    spread(HR, 2, p + 1, rmem, 9)

    for k in range(8):

        @pl.when(mine != k + 1)
        def _():
            rcopy(CB.at[k + 1], CB.at[k + 1], y_s.at[0, 0], y_r.at[k + 1], (c, p)).wait_recv()

    @pl.when((p > 0) & jnp.logical_not((y == 3) & (h == 1)))
    def _():
        rcopy(CB.at[0], CB.at[0], y_s.at[0, 0], y_r.at[0], (c, p)).wait_recv()

    @pl.when((p < 7) & jnp.logical_not((y == 0) & (h == 0)))
    def _():
        rcopy(CB.at[9], CB.at[9], y_s.at[0, 0], y_r.at[9], (c, p)).wait_recv()

    for k in range(1, 8):
        rcopy(RB.at[1, pp[k]], RB.at[1, pp[k]], rs_s.at[1, 1], rs_r.at[1, pp[k]], (c, p)).wait_recv()
    for b, pred in ((0, c > 0), (2, c < 63)):

        @pl.when(pred)
        def _():
            for k in range(8):
                rcopy(RB.at[b, k], RB.at[b, k], rs_s.at[b, 0], rs_r.at[b, k], (c, p)).wait_recv()

    row_sends(True)
    col_sends(True)


class Net:
    def __init__(self):
        self.sent = []

    def start(self, src, dst, s, r, dev):
        cp = rcopy(src, dst, s, r, dev)
        cp.start()
        self.sent.append(cp)

    def finish(self):
        for cp in self.sent:
            cp.wait_send()


class Ring:
    def __init__(self, net, arrs, place, ss, rs, ps, pr):
        self.net, self.arrs = net, arrs
        self.c, self.p, zh, _, _, self.h = place
        self.partner = (self.c + 1 - 2 * self.h, self.p)
        self.nxt = [at_z(self.c, zh, self.p, d) for d in (1, -1)]
        self.ss, self.rs, self.ps, self.pr = ss, rs, ps, pr

    def part(self, i, shard, lanes=None, h=None):
        src, out = self.arrs[i]
        h = self.h if h is None else h
        r = src.shape[0]
        hr = r // 2
        row = pl.ds(pl.multiple_of(shard * r + h * hr, hr), hr)
        return out.at[row, :] if lanes is None else out.at[row, lanes]

    def shard(self, t, di):
        return (self.p - t * (1, -1)[di] + 8) % 8

    def last(self, i, di):
        if i == di:
            return pl.ds(0, self.arrs[i][0].shape[1])
        if i < 2:
            return None
        w = self.arrs[i][0].shape[1] // 2
        return pl.ds(di * w, w)

    def first(self, i):
        src, _ = self.arrs[i]
        hr = src.shape[0] // 2
        for di in range(2):
            self.net.start(
                src.at[pl.ds(pl.multiple_of(self.h * hr, hr), hr), :],
                self.part(i, self.p),
                self.ss.at[di, 0, i],
                self.rs.at[di, 0, i],
                self.nxt[di],
            )

    def got(self, ref, s, r):
        rcopy(ref, ref, s, r, self.partner).wait_recv()

    def hop(self, i, t):
        for di in range(2):
            here = self.part(i, self.shard(t, di))
            self.got(here, self.ss.at[di, t - 1, i], self.rs.at[di, t - 1, i])
            ref = here
            if t == 3:
                lanes = self.last(i, di)
                ref = None if lanes is None else self.part(i, self.shard(t, di), lanes)
            if ref is not None:
                self.net.start(ref, ref, self.ss.at[di, t, i], self.rs.at[di, t, i], self.nxt[di])
            k = (t - 1) * 2 + di
            self.net.start(here, here, self.ps.at[k, i], self.pr.at[k, i], self.partner)

    def far(self, i):
        for di in range(2):
            lanes = self.last(i, di)
            if lanes is not None:
                ref = self.part(i, self.shard(4, 0), lanes)
                self.got(ref, self.ss.at[di, 3, i], self.rs.at[di, 3, i])
        here = self.part(i, self.shard(4, 0))
        self.net.start(here, here, self.ps.at[6, i], self.pr.at[6, i], self.partner)

    def done(self, i):
        for k in range(7):
            shard = self.shard(k // 2 + 1, k % 2) if k < 6 else self.shard(4, 0)
            ref = self.part(i, shard, h=1 - self.h)
            self.got(ref, self.ps.at[k, i], self.pr.at[k, i])


class Gather:
    def __init__(self, net, kv, place, ss, rs, ps, pr):
        self.net, self.kv = net, kv
        c, p, zh, x, y, h = place
        self.ss, self.rs, self.ps, self.pr = ss, rs, ps, pr
        self.partner = (c + 1 - 2 * h, p)
        self.ap = (ctx_of(zh, (x + 1 - h) % 4, (y + h) % 4, h), p)
        self.am = (ctx_of(zh, (x + 3 + h) % 4, (y + 4 - h) % 4, h), p)
        self.bp = (ctx_of(zh, (x + h) % 4, (y + 1 - h) % 4, h), p)
        self.bm = (ctx_of(zh, (x + 4 - h) % 4, (y + 3 + h) % 4, h), p)

    def slot(self, g, j, m, r=0):
        return self.kv.at[((g * 4 + j) * 2 + r) * 4 + m]

    def half(self, g, j, m, k):
        return self.kv.at[((g * 4 + j) * 2) * 4 + m, pl.ds(k * HB, HB), :]

    def got(self, ref, k):
        rcopy(ref, ref, self.ss.at[k], self.rs.at[k], self.partner).wait_recv()

    def send(self, src, dst, k, dev):
        self.net.start(src, dst, self.ss.at[k], self.rs.at[k], dev)

    def to_b(self, g, j, src=None):
        src = self.slot(g, j, 0) if src is None else src
        k = 20 * g + 4 + 4 * j
        self.send(src, self.slot(g, j, 1), k, self.bp)
        self.send(src, self.slot(g, j, 2), k + 1, self.bm)

    def to_partner(self, g, j, m, src=None):
        src = self.slot(g, j, m) if src is None else src
        k = 16 * g + 4 * j + m
        self.net.start(src, self.slot(g, j, m, 1), self.ps.at[k], self.pr.at[k], self.partner)

    def own(self, g, src=None):
        a = self.slot(g, 0, 0) if src is None else src
        self.send(a, self.slot(g, 1, 0), 20 * g, self.ap)
        self.send(a, self.slot(g, 2, 0), 20 * g + 1, self.am)
        self.to_b(g, 0, src)
        self.to_partner(g, 0, 0, src)

    def a_near(self, g):
        for j, k, dev in ((1, 0, self.ap), (2, 1, self.am)):
            self.got(self.slot(g, j, 0), 20 * g + k)
            self.send(self.half(g, j, 0, k), self.half(g, 3, 0, k), 20 * g + 2 + k, dev)
            self.to_b(g, j)
            self.to_partner(g, j, 0)

    def a_far(self, g):
        for k in range(2):
            self.got(self.half(g, 3, 0, k), 20 * g + 2 + k)
        self.to_b(g, 3)
        self.to_partner(g, 3, 0)

    def b_near(self, g, j):
        base = 20 * g + 4 + 4 * j
        for m, k, dev in ((1, 0, self.bp), (2, 1, self.bm)):
            self.got(self.slot(g, j, m), base + k)
            self.send(self.half(g, j, m, k), self.half(g, j, 3, k), base + 2 + k, dev)
            self.to_partner(g, j, m)

    def b_far(self, g, j):
        base = 20 * g + 4 + 4 * j
        for k in range(2):
            self.got(self.half(g, j, 3, k), base + 2 + k)
        self.to_partner(g, j, 3)

    def from_partner(self, g, j):
        for m in range(4):
            k = 16 * g + 4 * j + m
            ref = self.slot(g, j, m, 1)
            rcopy(ref, ref, self.ps.at[k], self.pr.at[k], self.partner).wait_recv()


def front_kernel(
    tok, wk, wv, wq, wo, gain, wpair,
    seq, RB, CB,
    WK, WV, WQ, WO, kv, blk, q, acc, high, mixed, rb, cb, HM, HL, HR,
    wss, wrs, wps, wpr, kss, krs, kps, kpr, zs, zr, ls, hello,
    rs_s, rs_r, z_s, z_r, x_s, x_r, y_s, y_r, els,
):
    place = coords()
    c, p, zh, x, y, h = place
    net = Net()
    arrs = ((wk, WK), (wv, WV), (wq, WQ), (wo, WO))
    ring = Ring(net, arrs, place, wss, wrs, wps, wpr)
    kvs = Gather(net, kv, place, kss, krs, kps, kpr)
    enter(ring.nxt + [ring.partner, kvs.ap, kvs.am, kvs.bp, kvs.bm])
    for i in range(3):
        ring.first(i)
    locs = []
    for i, (src, out) in enumerate(arrs):
        r = src.shape[0]
        cp = pltpu.make_async_copy(src, out.at[pl.ds(pl.multiple_of(p * r, r), r), :], ls.at[i])
        cp.start()
        locs.append(cp)

    for t in (1, 2, 3):
        ring.hop(0, t)
        ring.hop(1, t)
    ring.far(0)
    ring.far(1)
    pl.semaphore_signal(hello, inc=1, device_id=at_z(c, zh, p, -4), device_id_type=MESH)
    ring.hop(2, 1)
    locs[0].wait()
    locs[1].wait()
    ring.done(0)
    ring.done(1)
    t = tok[...]
    blk[0:128, :] = jnp.dot(t, WK[...], preferred_element_type=F32).astype(BF)
    v = jnp.dot(t, WV[...], preferred_element_type=F32)
    blk[128:256, :] = v[:, :128].astype(BF)
    blk[256:320, :] = jnp.concatenate([v[0:64, 128:192], v[64:128, 128:192]], axis=1).astype(BF)

    kvs.own(0, blk)
    loc = pltpu.make_async_copy(blk, kvs.slot(0, 0, 0), ls.at[4])
    loc.start()
    pl.semaphore_wait(hello, 1)
    flip = (c + 32 - 64 * zh, p)
    net.start(blk, kvs.slot(1, 0, 0), zs, zr, flip)
    ring.first(3)
    ring.hop(2, 2)
    kvs.a_near(0)
    kvs.b_near(0, 0)
    ring.hop(2, 3)
    kvs.a_far(0)
    kvs.b_far(0, 0)
    kvs.b_near(0, 1)
    kvs.b_near(0, 2)
    ring.far(2)
    ring.hop(3, 1)
    kvs.b_near(0, 3)
    for j in (1, 2, 3):
        kvs.b_far(0, j)
    locs[2].wait()
    ring.done(2)
    qq = jnp.dot(tok[...], WQ[...], preferred_element_type=F32).astype(BF)
    for n in range(H):
        q[n * 128 : (n + 1) * 128, :] = qq[:, n * KEY : (n + 1) * KEY]
    acc[...] = jnp.zeros_like(acc)
    high[...] = jnp.full_like(high, -1e30)
    loc.wait()

    scale = KEY ** (-0.5) * 1.4426950408889634

    def attend(g, j):
        kvs.from_partner(g, j)
        part = kv[pl.ds((g * 4 + j) * 8, 8)]
        k = part[:, 0:128, :].reshape(1024, 128)
        v1 = part[:, 128:256, :].reshape(1024, 128)
        lo = part[:, 256:320, :].astype(F32)
        hi = pltpu.roll(lo.reshape(512, 128), 64, 1).reshape(8, 64, 128)
        v2 = jnp.concatenate([lo, hi], axis=1).reshape(1024, 128)
        lane = lax.broadcasted_iota(jnp.int32, (1024, 128), 1)
        v2 = jnp.where(lane == 64, 1.0, v2).astype(BF)
        m = high[:, 0:1]
        s = lax.dot_general(q[...], k, (((1,), (1,)), ((), ())), preferred_element_type=F32)
        m2 = jnp.maximum(m, jnp.max(s, axis=1, keepdims=True))
        w = jnp.exp2((s - m2) * scale).astype(BF)
        o = jnp.dot(w, jnp.concatenate([v1, v2], axis=1), preferred_element_type=F32)
        acc[...] = acc[...] * jnp.exp2((m - m2) * scale) + o
        high[...] = jnp.broadcast_to(m2, high.shape)

    attend(0, 0)
    ring.hop(3, 2)
    other = kvs.slot(1, 0, 0)
    rcopy(other, other, zs, zr, flip).wait_recv()
    kvs.own(1)
    attend(0, 1)
    kvs.a_near(1)
    kvs.b_near(1, 0)
    ring.hop(3, 3)
    kvs.a_far(1)
    attend(0, 2)
    kvs.b_far(1, 0)
    kvs.b_near(1, 1)
    kvs.b_near(1, 2)
    kvs.b_near(1, 3)
    ring.far(3)
    attend(0, 3)
    for j in (1, 2, 3):
        kvs.b_far(1, j)
    for j in range(4):
        attend(1, j)
    locs[3].wait()
    ring.done(3)

    a = acc[...]
    mx = (a[:, 0:VAL] / a[:, VAL : VAL + 1]).astype(BF)
    for n in range(H):
        mixed[:, n * VAL : (n + 1) * VAL] = mx[n * 128 : (n + 1) * 128, :]
    summed = tok[...].astype(F32) + jnp.dot(mixed[...], WO[...], preferred_element_type=F32)
    seq[...] = summed.astype(BF)
    pooled = jnp.mean(summed.reshape(8, POOL, summed.shape[1]), axis=1)
    ms = jnp.mean(pooled * pooled, axis=-1, keepdims=True)
    normed = (pooled * lax.rsqrt(ms + 1e-06) * gain[...]).astype(BF)
    both = jnp.dot(normed, wpair[...], preferred_element_type=F32).astype(BF)
    rb[...] = both[:, :PC]
    cb[...] = both[:, PC:]
    exchange(rb, cb, RB, CB, HM, HL, HR, rs_s, rs_r, z_s, z_r, x_s, x_r, y_s, y_r, els)
    net.finish()


def front(tok, wk, wv, wq, wo, gain, wpair):
    vm = pl.BlockSpec(memory_space=pltpu.VMEM)
    dma = pltpu.SemaphoreType.DMA
    hold = pltpu.VMEM((8, 8, PC), BF)
    return pl.pallas_call(
        front_kernel,
        out_shape=(
            jax.ShapeDtypeStruct(tok.shape, BF),
            jax.ShapeDtypeStruct((3, 8, 8, PC), BF),
            jax.ShapeDtypeStruct((10, 8, 8, PC), BF),
        ),
        in_specs=[vm] * 7,
        out_specs=(vm,) * 3,
        scratch_shapes=[pltpu.VMEM((8 * w.shape[0], w.shape[1]), BF) for w in (wk, wv, wq, wo)]
        + [
            pltpu.VMEM((64, BR, 128), BF),
            pltpu.VMEM((BR, 128), BF),
            pltpu.VMEM((512, 128), BF),
            pltpu.VMEM((512, 256), F32),
            pltpu.VMEM((512, 128), F32),
            pltpu.VMEM((128, H * VAL), BF),
            pltpu.VMEM((8, PC), BF),
            pltpu.VMEM((8, PC), BF),
            hold,
            hold,
            hold,
        ]
        + [dma((2, 4, 4)), dma((2, 4, 4)), dma((7, 4)), dma((7, 4))]
        + [dma((40,)), dma((40,)), dma((32,)), dma((32,)), dma, dma, dma((5,))]
        + [pltpu.SemaphoreType.REGULAR]
        + [dma((3, 8)), dma((3, 8)), dma((3, 2)), dma((3, 8)), dma((3, 3)), dma((3,)), dma((3, 7)), dma((10,)), dma((7,))],
        compiler_params=pltpu.CompilerParams(
            collective_id=0, has_side_effects=True, vmem_limit_bytes=VMEM_LIMIT
        ),
        name="front",
    )(tok, wk, wv, wq, wo, gain, wpair)


def conv_kernel(rb, cb, w, seq_in, out, seq_out):
    seq_out[...] = seq_in[...]

    def seq(s, carry):
        prev = rb[0, pl.ds(s, 1)].reshape(8, PC).astype(F32)
        own = rb[1, pl.ds(s, 1)].reshape(8, PC).astype(F32)
        nxt = rb[2, pl.ds(s, 1)].reshape(8, PC).astype(F32)
        col = jnp.concatenate([cb[k, pl.ds(s, 1)].reshape(8, PC) for k in range(10)], axis=0).astype(F32)
        rows = [prev[6:7], prev[7:8]] + [own[k : k + 1] for k in range(8)] + [nxt[0:1], nxt[1:2]]
        shifted = [col[6 + 2 * b : 70 + 2 * b] for b in range(3)]
        maps = [[(r * cs).astype(BF) for r in rows] for cs in shifted]
        for i in range(8):
            lhs = jnp.concatenate(
                [maps[b][i + 2 * a] for a in range(3) for b in range(3)], axis=1
            )
            t = jnp.dot(lhs, w[...], preferred_element_type=F32)
            res = maps[1][i + 2].astype(F32) + jax.nn.gelu(t)
            out[pl.ds(s, 1), i] = res.astype(BF).reshape(1, 64, PC)
        return carry

    lax.fori_loop(0, 8, seq, 0)


def convolve(rb, cb, w, seq):
    vm = pl.BlockSpec(memory_space=pltpu.VMEM)
    return pl.pallas_call(
        conv_kernel,
        out_shape=(jax.ShapeDtypeStruct((8, 8, 64, PC), BF), jax.ShapeDtypeStruct(seq.shape, BF)),
        in_specs=[vm] * 4,
        out_specs=(vm, vm),
        compiler_params=pltpu.CompilerParams(vmem_limit_bytes=VMEM_LIMIT),
        name="convolve",
    )(rb, cb, w, seq)


def on_device(tokens, w_query, w_key, w_value, w_out, norm_gain, w_pair, conv_weight):
    tok = tokens.reshape(tokens.shape[1], tokens.shape[2])
    seq, rb, cb = front(tok, w_key, w_value, w_query, w_out, norm_gain.reshape(1, -1), w_pair)
    out, seq = convolve(rb, cb, conv_weight.reshape(9 * PC, PC), seq)
    return seq.reshape(tokens.shape), out


def solution(mesh):
    return jax.shard_map(
        on_device,
        mesh=mesh,
        in_specs=(
            P("pair", "ctx", None),
            P("pair", None),
            P("pair", None),
            P("pair", None),
            P("pair", None),
            P(),
            P(),
            P(),
        ),
        out_specs=(P("pair", "ctx", None), P(None, "ctx", "pair", None)),
        check_vma=False,
    )
```

time: 1520 us -> 108 us (0.07); the launches traced: 1490 us -> 107 us
  waiting for transfers between devices: 1290 us -> 0 us
  blocking collectives: 131 us -> 0 us
  Pallas kernels: 0 us -> 105 us
  matrix products: 31 us -> 0 us
    all_gather x5 -> x0, waiting for transfers between devices: 1280 us -> none  [the longest x1 1030 us: on_device(): gathered = lax.all_gather(colpart, ('ctx', 'pair'), axis=1, tiled=True)]
    all_gather x3 -> x0, blocking collectives: 131 us -> none  [the longest x1 47 us: on_device(): lax.all_gather(w_value, 'pair', axis=0, tiled=True)]
    pallas_call x0 -> x2, Pallas kernels: none -> 105 us  [the longest x1 98.7 us: front(): pl.pallas_call(front_kernel, out_shape=(jax.ShapeDtypeStruct(tok.shape, B...]
    dot_general x16 -> x0, matrix products: 31 us -> none  [the longest x1 9.71 us: on_device(): jnp.einsum('bhqn,bnv->bhqv', weights.astype(jnp.bfloat16), value_piece, p...]
  transfers between devices with their start and end apart: 9 -> 0, of which waited for: 7 -> 0; matrix products, arithmetic and copies ran while one was open for 2% -> 0% of each run, Pallas kernels for 0% -> 0%
where the time goes in v2:
time: 108 us; the launch traced here: 107 us
  Pallas kernels  105 us (97%)
  local copies, waits for them, and re-layouts  1.29 us (1%)
    pallas_call x1, Pallas kernels, front(): pl.pallas_call(front_kernel, out_shape=(jax.ShapeDtypeStruct(tok.shape, B...  98.7 us
    pallas_call x1, Pallas kernels, convolve(): pl.pallas_call(conv_kernel, out_shape=(jax.ShapeDtypeStruct((8, 8, 64, PC...  6.29 us

profile of v2, /device:TPU:1, one launch (start us, length us, event | category | flops | bytes accessed | tf_op | source)
XLA Modules:
  0.0 107.0 jit_solution(99557077042996502)
XLA Ops:
  0.6 1.3 %reshape.17.gain = f32[1,1536]{1,0:T(1,128)} reshape(f32[1536]{0:T(1024)} %param.13) | data formatting | bytes 12288 | tf_op jit(solution)/shard_map/reshape | solution.py:559
  1.9 98.7 %front.1 = (bf16[128,1536]{1,0:T(8,128)(2,1)}, bf16[3,8,8,128]{3,2,1,0:T(8,128)(2,1)}, bf16[10,8,8,128]{3,2,1,0:T(8,128)(2,1)}) custom-call(bf16[128,1536]{1,0:T(8,128)(2,1)} %bitcast.3, bf16[192,128]{1,0:T(8,128)(2,1)} %wk.1, bf16[192,192]{1,0:T(8,128)(2,1)} %wv.1, bf16[192,512]{1,0:T(8,128)(2,1)} %wq.1, bf16[96,1536]{1,0:T(8,128)(2,1)} %wo.1, ...), custom_call_target="tpu_custom_call" | custom-call | tf_op jit(solution)/shard_map/front/pallas_call | solution.py:488
  100.7 6.3 %convolve.1 = (bf16[8,8,64,128]{3,2,1,0:T(8,128)(2,1)}, bf16[128,1536]{1,0:T(8,128)(2,1)}) custom-call(bf16[3,8,8,128]{3,2,1,0:T(8,128)(2,1)} %get-tuple-element.7.rb, bf16[10,8,8,128]{3,2,1,0:T(8,128)(2,1)} %get-tuple-element.8.cb, bf16[1152,128]{1,0:T(8,128)(2,1)} %bitcast.4, bf16[128,1536]{1,0:T(8,128)(2,1)} %get-tuple-element.9.seq_in), custom_call_target="tpu_custom_call" | custom-call | tf_op jit(solution)/shard_map/convolve/pallas_call | solution.py:547

commit v3 on v2

--- a/solution.py
+++ b/solution.py
@@ -48,12 +48,10 @@
     pl.semaphore_wait(barrier, len(devs))
 
 
-def exchange(rb, cb, RB, CB, HM, HL, HR, rs_s, rs_r, z_s, z_r, x_s, x_r, y_s, y_r, ls):
+def exchange(rb, cb, RB, CB, HM, HL, HR, rs_s, rs_r, z_s, z_r, y_s, y_r, ls):
     c, p, zh, x, y, h = coords()
-    flip = c + 32 - 64 * zh
     cn, cv = (c + 1) % 64, (c + 63) % 64
     pp = [(p + k) % 8 for k in range(8)]
-    xs = [(ctx_of(zh, (x + k) % 4, y, h), p) for k in (1, 2, 3)]
     yc = []
     for k in range(4):
         for e in range(2):
@@ -65,29 +63,34 @@
         cp.start()
         cp.wait()
 
-    tgt = c // 8
-    jobs = [(tgt, HM, 0, None), (tgt + 1, HL, 1, (c % 8 == 7) & (tgt < 7)), (tgt - 1, HR, 2, (c % 8 == 0) & (tgt > 0))]
-
     def cond(pred, fn):
         if pred is None:
             fn()
         else:
             pl.when(pred)(fn)
 
+    tgt = c // 8
+    jobs = [
+        (tgt, HM, 0, None),
+        (tgt + 1, HL, 1, (c % 8 == 7) & (tgt < 7)),
+        (tgt - 1, HR, 2, (c % 8 == 0) & (tgt > 0)),
+    ]
+
     def col_sends(wait):
         for t, buf, b, pred in jobs:
-            for f in range(2):
-                dc = c if f == 0 else flip
-
-                def go(t=t, buf=buf, b=b, f=f, dc=dc):
-                    cp = rcopy(cb, buf.at[p], z_s.at[b, f], z_r.at[b, p], (dc, t))
-                    cp.wait_send() if wait else cp.start()
-
-                if f == 1:
-                    cond(pred, go)
-                else:
-                    away = t != p
-                    cond(away if pred is None else away & pred, go)
+            for f in (1, 0):
+                for k in (2, 1, 3, 0):
+                    dc = ctx_of(zh if f == 0 else 1 - zh, (x + k) % 4, y, h)
+
+                    def go(t=t, buf=buf, b=b, n=4 * f + k, dc=dc):
+                        cp = rcopy(cb, buf.at[p], z_s.at[b, n], z_r.at[b, p], (dc, t))
+                        cp.wait_send() if wait else cp.start()
+
+                    if f or k:
+                        cond(pred, go)
+                    else:
+                        away = t != p
+                        cond(away if pred is None else away & pred, go)
 
     col_sends(False)
     for t, buf, b, pred in jobs:
@@ -125,46 +128,26 @@
     def _():
         CB[9] = jnp.zeros((8, 8, PC), BF)
 
-    def spread(buf, b, owner, member, cslot):
-        ox = owner % 4
-        oz = owner // 4
-        holder = member & (x == ox)
-
-        @pl.when(holder)
-        def _():
-            for s in range(8):
-
-                @pl.when((s != p) | (zh != oz))
+    mine = 1 + 2 * y + h
+    spreads = (
+        (HM, 0, p, None, mine),
+        (HL, 1, p - 1, (y == 3) & (h == 1) & (p > 0), 0),
+        (HR, 2, p + 1, (y == 0) & (h == 0) & (p < 7), 9),
+    )
+    for buf, b, owner, member, cslot in spreads:
+
+        def take(buf=buf, b=b, owner=owner, cslot=cslot):
+            for n in range(8):
+
+                @pl.when((p != n) | (zh != owner // 4) | (x != owner % 4))
                 def _():
-                    rcopy(buf.at[s], buf.at[s], z_s.at[b, 0], z_r.at[b, s], (c, p)).wait_recv()
-
-            for k in range(3):
-                rcopy(buf, buf, x_s.at[b, k], x_r.at[b], xs[k]).start()
-
-        @pl.when(member & (x != ox))
-        def _():
-            rcopy(buf, buf, x_s.at[b, 0], x_r.at[b], (c, p)).wait_recv()
-
-        @pl.when(member)
-        def _():
+                    rcopy(buf.at[n], buf.at[n], z_s.at[b, 0], z_r.at[b, n], (c, p)).wait_recv()
+
             for k in range(7):
                 rcopy(buf, CB.at[cslot], y_s.at[b, k], y_r.at[cslot], yc[k]).start()
             local(buf, CB.at[cslot], 4 + b)
-            for k in range(7):
-                rcopy(buf, CB.at[cslot], y_s.at[b, k], y_r.at[cslot], yc[k]).wait_send()
-
-        @pl.when(holder)
-        def _():
-            for k in range(3):
-                rcopy(buf, buf, x_s.at[b, k], x_r.at[b], xs[k]).wait_send()
-
-    always = c >= 0
-    mine = 1 + 2 * y + h
-    lmem = (y == 3) & (h == 1) & (p > 0)
-    rmem = (y == 0) & (h == 0) & (p < 7)
-    spread(HM, 0, p, always, mine)
-    spread(HL, 1, p - 1, lmem, 0)
-    spread(HR, 2, p + 1, rmem, 9)
+
+        cond(member, take)
 
     for k in range(8):
 
@@ -191,6 +174,13 @@
 
     row_sends(True)
     col_sends(True)
+    for buf, b, owner, member, cslot in spreads:
+
+        def sent(buf=buf, b=b, cslot=cslot):
+            for k in range(7):
+                rcopy(buf, CB.at[cslot], y_s.at[b, k], y_r.at[cslot], yc[k]).wait_send()
+
+        cond(member, sent)
 
 
 class Net:
@@ -207,75 +197,104 @@
             cp.wait_send()
 
 
-class Ring:
-    def __init__(self, net, arrs, place, ss, rs, ps, pr):
+DIST = (1, -1, 2, -2, 3, -3, 4)
+
+
+class Weights:
+    def __init__(self, net, arrs, place, zs, zr, ns, nr, ps, pr):
         self.net, self.arrs = net, arrs
-        self.c, self.p, zh, _, _, self.h = place
+        self.c, self.p, self.zh, x, y, self.h = place
+        self.color = (x + y) % 2
         self.partner = (self.c + 1 - 2 * self.h, self.p)
-        self.nxt = [at_z(self.c, zh, self.p, d) for d in (1, -1)]
-        self.ss, self.rs, self.ps, self.pr = ss, rs, ps, pr
-
-    def part(self, i, shard, lanes=None, h=None):
+        self.plane = [
+            (ctx_of(self.zh, (x + dx) % 4, (y + dy) % 4, self.h), self.p)
+            for dx, dy in ((1, 0), (3, 0), (0, 1), (0, 3))
+        ]
+        self.zs, self.zr, self.ns, self.nr, self.ps, self.pr = zs, zr, ns, nr, ps, pr
+
+    def at(self, d):
+        return at_z(self.c, self.zh, self.p, d)
+
+    def quarter(self, i, base, h, color, side=None):
+        src, _ = self.arrs[i]
+        r, w = src.shape
+        if i < 3:
+            n = r // 4
+            row, lane, wide = base + h * 2 * n + color * n, 0, w
+        else:
+            n = r // 2
+            row, lane, wide = base + h * n, pl.multiple_of(color * (w // 2), w // 2), w // 2
+        if side is not None:
+            wide = wide // 2
+            lane = lane + side * wide
+            if i == 3:
+                lane = pl.multiple_of(lane, wide)
+        return pl.ds(pl.multiple_of(row, n), n), pl.ds(lane, wide)
+
+    def own(self, i, side=None):
+        rows, lanes = self.quarter(i, 0, self.h, self.color, side)
+        return self.arrs[i][0].at[rows, lanes]
+
+    def part(self, i, m, flip_h=0, flip_c=0, side=None, d=None):
         src, out = self.arrs[i]
-        h = self.h if h is None else h
-        r = src.shape[0]
-        hr = r // 2
-        row = pl.ds(pl.multiple_of(shard * r + h * hr, hr), hr)
-        return out.at[row, :] if lanes is None else out.at[row, lanes]
-
-    def shard(self, t, di):
-        return (self.p - t * (1, -1)[di] + 8) % 8
-
-    def last(self, i, di):
-        if i == di:
-            return pl.ds(0, self.arrs[i][0].shape[1])
-        if i < 2:
-            return None
-        w = self.arrs[i][0].shape[1] // 2
-        return pl.ds(di * w, w)
+        d = DIST[m] if d is None else d
+        base = ((self.p - d + 8) % 8) * src.shape[0]
+        h = 1 - self.h if flip_h else self.h
+        color = 1 - self.color if flip_c else self.color
+        rows, lanes = self.quarter(i, base, h, color, side)
+        return out.at[rows, lanes]
+
+    def got(self, ref, sem):
+        rcopy(ref, ref, sem, sem, self.partner).wait_recv()
+
+    def direct(self):
+        for m in (6, 4, 5, 2, 3, 0, 1):
+            for i in range(2):
+                d = DIST[m] if m < 6 else (4, -4)[i]
+                dst = self.part(i, m, d=0)
+                self.net.start(self.own(i), dst, self.zs.at[i, m], self.zr.at[i, m], self.at(d))
 
     def first(self, i):
-        src, _ = self.arrs[i]
-        hr = src.shape[0] // 2
-        for di in range(2):
-            self.net.start(
-                src.at[pl.ds(pl.multiple_of(self.h * hr, hr), hr), :],
-                self.part(i, self.p),
-                self.ss.at[di, 0, i],
-                self.rs.at[di, 0, i],
-                self.nxt[di],
-            )
-
-    def got(self, ref, s, r):
-        rcopy(ref, ref, s, r, self.partner).wait_recv()
+        for di, d in enumerate((1, -1)):
+            dst = self.part(i, di, d=0)
+            self.net.start(self.own(i), dst, self.zs.at[i, di], self.zr.at[i, di], self.at(d))
+
+    def spread(self, i, m):
+        ref = self.part(i, m)
+        self.net.start(ref, ref, self.ps.at[i, m], self.pr.at[i, m], self.partner)
+        to = self.plane[m % 4]
+        self.net.start(ref, ref, self.ns.at[i, m], self.nr.at[i, m], to)
+
+    def take(self, i, m):
+        self.got(self.part(i, m), self.zr.at[i, m])
+        self.spread(i, m)
 
     def hop(self, i, t):
-        for di in range(2):
-            here = self.part(i, self.shard(t, di))
-            self.got(here, self.ss.at[di, t - 1, i], self.rs.at[di, t - 1, i])
-            ref = here
-            if t == 3:
-                lanes = self.last(i, di)
-                ref = None if lanes is None else self.part(i, self.shard(t, di), lanes)
-            if ref is not None:
-                self.net.start(ref, ref, self.ss.at[di, t, i], self.rs.at[di, t, i], self.nxt[di])
-            k = (t - 1) * 2 + di
-            self.net.start(here, here, self.ps.at[k, i], self.pr.at[k, i], self.partner)
+        for di, d in enumerate((1, -1)):
+            m = (t - 1) * 2 + di
+            self.got(self.part(i, m), self.zr.at[i, m])
+            side = di if t == 3 else None
+            ref = self.part(i, m, side=side)
+            n = m + 2
+            self.net.start(ref, ref, self.zs.at[i, n], self.zr.at[i, n], self.at(d))
+            self.spread(i, m)
 
     def far(self, i):
         for di in range(2):
-            lanes = self.last(i, di)
-            if lanes is not None:
-                ref = self.part(i, self.shard(4, 0), lanes)
-                self.got(ref, self.ss.at[di, 3, i], self.rs.at[di, 3, i])
-        here = self.part(i, self.shard(4, 0))
-        self.net.start(here, here, self.ps.at[6, i], self.pr.at[6, i], self.partner)
+            self.got(self.part(i, 6, side=di), self.zr.at[i, 6 + di])
+        self.spread(i, 6)
+
+    def near(self, i):
+        for m in range(7):
+            ref = self.part(i, m, flip_c=1)
+            self.got(ref, self.nr.at[i, m])
+            self.net.start(ref, ref, self.ps.at[i, 7 + m], self.pr.at[i, 7 + m], self.partner)
 
     def done(self, i):
-        for k in range(7):
-            shard = self.shard(k // 2 + 1, k % 2) if k < 6 else self.shard(4, 0)
-            ref = self.part(i, shard, h=1 - self.h)
-            self.got(ref, self.ps.at[k, i], self.pr.at[k, i])
+        for m in range(7):
+            self.got(self.part(i, m, flip_h=1), self.pr.at[i, m])
+        for m in range(7):
+            self.got(self.part(i, m, flip_h=1, flip_c=1), self.pr.at[i, 7 + m])
 
 
 class Gather:
@@ -353,37 +372,44 @@
 
 
 def front_kernel(
-    tok, wk, wv, wq, wo, gain, wpair,
+    tok_hbm, wk, wv, wq, wo, gain, wpair_hbm,
     seq, RB, CB,
-    WK, WV, WQ, WO, kv, blk, q, acc, high, mixed, rb, cb, HM, HL, HR,
-    wss, wrs, wps, wpr, kss, krs, kps, kpr, zs, zr, ls, hello,
-    rs_s, rs_r, z_s, z_r, x_s, x_r, y_s, y_r, els,
+    WK, WV, WQ, WO, tok, wpair, kv, blk, q, acc, high, mixed, rb, cb, HM, HL, HR,
+    wzs, wzr, wns, wnr, wps, wpr, kss, krs, kps, kpr, zs, zr, ls, hello,
+    rs_s, rs_r, z_s, z_r, y_s, y_r, els,
 ):
     place = coords()
     c, p, zh, x, y, h = place
     net = Net()
     arrs = ((wk, WK), (wv, WV), (wq, WQ), (wo, WO))
-    ring = Ring(net, arrs, place, wss, wrs, wps, wpr)
+    ring = Weights(net, arrs, place, wzs, wzr, wns, wnr, wps, wpr)
     kvs = Gather(net, kv, place, kss, krs, kps, kpr)
-    enter(ring.nxt + [ring.partner, kvs.ap, kvs.am, kvs.bp, kvs.bm])
-    for i in range(3):
-        ring.first(i)
+    near = [ring.at(d) for d in (1, -1, 2, -2, 3, -3, 4, -4)]
+    enter(near + ring.plane + [ring.partner])
+    ring.direct()
+    ring.first(2)
+    pl.semaphore_signal(hello, inc=1, device_id=ring.at(-4), device_id_type=MESH)
     locs = []
     for i, (src, out) in enumerate(arrs):
         r = src.shape[0]
-        cp = pltpu.make_async_copy(src, out.at[pl.ds(pl.multiple_of(p * r, r), r), :], ls.at[i])
+        locs.append((src, out.at[pl.ds(pl.multiple_of(p * r, r), r), :]))
+    locs += [(tok_hbm, tok), (wpair_hbm, wpair)]
+    locs = [pltpu.make_async_copy(src, dst, ls.at[i]) for i, (src, dst) in enumerate(locs)]
+    for cp in locs:
         cp.start()
-        locs.append(cp)
-
-    for t in (1, 2, 3):
-        ring.hop(0, t)
-        ring.hop(1, t)
-    ring.far(0)
-    ring.far(1)
-    pl.semaphore_signal(hello, inc=1, device_id=at_z(c, zh, p, -4), device_id_type=MESH)
+
+    for m in range(4):
+        ring.take(0, m)
+        ring.take(1, m)
     ring.hop(2, 1)
-    locs[0].wait()
-    locs[1].wait()
+    for m in range(4, 7):
+        ring.take(0, m)
+        ring.take(1, m)
+    ring.hop(2, 2)
+    for i in (0, 1, 4):
+        locs[i].wait()
+    ring.near(0)
+    ring.near(1)
     ring.done(0)
     ring.done(1)
     t = tok[...]
@@ -392,33 +418,28 @@
     blk[128:256, :] = v[:, :128].astype(BF)
     blk[256:320, :] = jnp.concatenate([v[0:64, 128:192], v[64:128, 128:192]], axis=1).astype(BF)
 
-    kvs.own(0, blk)
-    loc = pltpu.make_async_copy(blk, kvs.slot(0, 0, 0), ls.at[4])
-    loc.start()
     pl.semaphore_wait(hello, 1)
     flip = (c + 32 - 64 * zh, p)
     net.start(blk, kvs.slot(1, 0, 0), zs, zr, flip)
+    kvs.own(0, blk)
+    loc = pltpu.make_async_copy(blk, kvs.slot(0, 0, 0), ls.at[6])
+    loc.start()
+    acc[...] = jnp.zeros_like(acc)
+    high[...] = jnp.full_like(high, -1e30)
+    ring.hop(2, 3)
+    kvs.a_near(0)
+    ring.far(2)
+    kvs.b_near(0, 0)
+    ring.near(2)
     ring.first(3)
-    ring.hop(2, 2)
-    kvs.a_near(0)
-    kvs.b_near(0, 0)
-    ring.hop(2, 3)
     kvs.a_far(0)
     kvs.b_far(0, 0)
     kvs.b_near(0, 1)
-    kvs.b_near(0, 2)
-    ring.far(2)
-    ring.hop(3, 1)
-    kvs.b_near(0, 3)
-    for j in (1, 2, 3):
-        kvs.b_far(0, j)
     locs[2].wait()
     ring.done(2)
     qq = jnp.dot(tok[...], WQ[...], preferred_element_type=F32).astype(BF)
     for n in range(H):
         q[n * 128 : (n + 1) * 128, :] = qq[:, n * KEY : (n + 1) * KEY]
-    acc[...] = jnp.zeros_like(acc)
-    high[...] = jnp.full_like(high, -1e30)
     loc.wait()
 
     scale = KEY ** (-0.5) * 1.4426950408889634
@@ -441,28 +462,36 @@
         acc[...] = acc[...] * jnp.exp2((m - m2) * scale) + o
         high[...] = jnp.broadcast_to(m2, high.shape)
 
+    kvs.b_near(0, 2)
     attend(0, 0)
-    ring.hop(3, 2)
+    kvs.b_near(0, 3)
+    ring.hop(3, 1)
+    for j in (1, 2, 3):
+        kvs.b_far(0, j)
+    attend(0, 1)
     other = kvs.slot(1, 0, 0)
     rcopy(other, other, zs, zr, flip).wait_recv()
     kvs.own(1)
-    attend(0, 1)
+    ring.hop(3, 2)
+    attend(0, 2)
     kvs.a_near(1)
     kvs.b_near(1, 0)
+    kvs.a_far(1)
     ring.hop(3, 3)
-    kvs.a_far(1)
-    attend(0, 2)
+    attend(0, 3)
     kvs.b_far(1, 0)
     kvs.b_near(1, 1)
     kvs.b_near(1, 2)
+    attend(1, 0)
     kvs.b_near(1, 3)
     ring.far(3)
-    attend(0, 3)
     for j in (1, 2, 3):
         kvs.b_far(1, j)
-    for j in range(4):
+    ring.near(3)
+    for j in (1, 2, 3):
         attend(1, j)
     locs[3].wait()
+    locs[5].wait()
     ring.done(3)
 
     a = acc[...]
@@ -473,11 +502,11 @@
     seq[...] = summed.astype(BF)
     pooled = jnp.mean(summed.reshape(8, POOL, summed.shape[1]), axis=1)
     ms = jnp.mean(pooled * pooled, axis=-1, keepdims=True)
-    normed = (pooled * lax.rsqrt(ms + 1e-06) * gain[...]).astype(BF)
+    normed = (pooled * lax.rsqrt(ms + 1e-06) * gain[...].reshape(1, -1)).astype(BF)
     both = jnp.dot(normed, wpair[...], preferred_element_type=F32).astype(BF)
     rb[...] = both[:, :PC]
     cb[...] = both[:, PC:]
-    exchange(rb, cb, RB, CB, HM, HL, HR, rs_s, rs_r, z_s, z_r, x_s, x_r, y_s, y_r, els)
+    exchange(rb, cb, RB, CB, HM, HL, HR, rs_s, rs_r, z_s, z_r, y_s, y_r, els)
     net.finish()
 
 
@@ -485,6 +514,7 @@
     vm = pl.BlockSpec(memory_space=pltpu.VMEM)
     dma = pltpu.SemaphoreType.DMA
     hold = pltpu.VMEM((8, 8, PC), BF)
+    hbm = pl.BlockSpec(memory_space=pl.ANY)
     return pl.pallas_call(
         front_kernel,
         out_shape=(
@@ -492,10 +522,12 @@
             jax.ShapeDtypeStruct((3, 8, 8, PC), BF),
             jax.ShapeDtypeStruct((10, 8, 8, PC), BF),
         ),
-        in_specs=[vm] * 7,
+        in_specs=[hbm] * 5 + [vm, hbm],
         out_specs=(vm,) * 3,
         scratch_shapes=[pltpu.VMEM((8 * w.shape[0], w.shape[1]), BF) for w in (wk, wv, wq, wo)]
         + [
+            pltpu.VMEM(tok.shape, BF),
+            pltpu.VMEM(wpair.shape, BF),
             pltpu.VMEM((64, BR, 128), BF),
             pltpu.VMEM((BR, 128), BF),
             pltpu.VMEM((512, 128), BF),
@@ -508,10 +540,10 @@
             hold,
             hold,
         ]
-        + [dma((2, 4, 4)), dma((2, 4, 4)), dma((7, 4)), dma((7, 4))]
-        + [dma((40,)), dma((40,)), dma((32,)), dma((32,)), dma, dma, dma((5,))]
+        + [dma((4, 8)), dma((4, 8)), dma((4, 7)), dma((4, 7)), dma((4, 14)), dma((4, 14))]
+        + [dma((40,)), dma((40,)), dma((32,)), dma((32,)), dma, dma, dma((7,))]
         + [pltpu.SemaphoreType.REGULAR]
-        + [dma((3, 8)), dma((3, 8)), dma((3, 2)), dma((3, 8)), dma((3, 3)), dma((3,)), dma((3, 7)), dma((10,)), dma((7,))],
+        + [dma((3, 8)), dma((3, 8)), dma((3, 8)), dma((3, 8)), dma((3, 7)), dma((10,)), dma((7,))],
         compiler_params=pltpu.CompilerParams(
             collective_id=0, has_side_effects=True, vmem_limit_bytes=VMEM_LIMIT
         ),
@@ -519,8 +551,12 @@
     )(tok, wk, wv, wq, wo, gain, wpair)
 
 
-def conv_kernel(rb, cb, w, seq_in, out, seq_out):
-    seq_out[...] = seq_in[...]
+def conv_kernel(rb, cb, w, seq_in, out, seq_out, tile, line, sems):
+    bring = pltpu.make_async_copy(seq_in, line, sems.at[8])
+    bring.start()
+
+    def put(s):
+        return pltpu.make_async_copy(tile.at[s], out.at[s], sems.at[s])
 
     def seq(s, carry):
         prev = rb[0, pl.ds(s, 1)].reshape(8, PC).astype(F32)
@@ -529,26 +565,38 @@
         col = jnp.concatenate([cb[k, pl.ds(s, 1)].reshape(8, PC) for k in range(10)], axis=0).astype(F32)
         rows = [prev[6:7], prev[7:8]] + [own[k : k + 1] for k in range(8)] + [nxt[0:1], nxt[1:2]]
         shifted = [col[6 + 2 * b : 70 + 2 * b] for b in range(3)]
-        maps = [[(r * cs).astype(BF) for r in rows] for cs in shifted]
-        for i in range(8):
-            lhs = jnp.concatenate(
-                [maps[b][i + 2 * a] for a in range(3) for b in range(3)], axis=1
-            )
-            t = jnp.dot(lhs, w[...], preferred_element_type=F32)
-            res = maps[1][i + 2].astype(F32) + jax.nn.gelu(t)
-            out[pl.ds(s, 1), i] = res.astype(BF).reshape(1, 64, PC)
+        maps = [jnp.concatenate([(r * cs).astype(BF) for r in rows], axis=0) for cs in shifted]
+        lhs = jnp.concatenate(
+            [maps[b][128 * a : 128 * a + 512] for a in range(3) for b in range(3)], axis=1
+        )
+        t = jnp.dot(lhs, w[...], preferred_element_type=F32)
+        res = maps[1][128:640].astype(F32) + jax.nn.gelu(t)
+        tile[pl.ds(s, 1)] = res.astype(BF).reshape(1, 8, 64, PC)
+        put(s).start()
         return carry
 
     lax.fori_loop(0, 8, seq, 0)
+    bring.wait()
+    give = pltpu.make_async_copy(line, seq_out, sems.at[8])
+    give.start()
+    for s in range(8):
+        put(s).wait()
+    give.wait()
 
 
 def convolve(rb, cb, w, seq):
     vm = pl.BlockSpec(memory_space=pltpu.VMEM)
+    hbm = pl.BlockSpec(memory_space=pl.ANY)
     return pl.pallas_call(
         conv_kernel,
         out_shape=(jax.ShapeDtypeStruct((8, 8, 64, PC), BF), jax.ShapeDtypeStruct(seq.shape, BF)),
-        in_specs=[vm] * 4,
-        out_specs=(vm, vm),
+        in_specs=[vm] * 3 + [hbm],
+        out_specs=(hbm, hbm),
+        scratch_shapes=[
+            pltpu.VMEM((8, 8, 64, PC), BF),
+            pltpu.VMEM(seq.shape, BF),
+            pltpu.SemaphoreType.DMA((9,)),
+        ],
         compiler_params=pltpu.CompilerParams(vmem_limit_bytes=VMEM_LIMIT),
         name="convolve",
     )(rb, cb, w, seq)
@@ -556,7 +604,7 @@
 
 def on_device(tokens, w_query, w_key, w_value, w_out, norm_gain, w_pair, conv_weight):
     tok = tokens.reshape(tokens.shape[1], tokens.shape[2])
-    seq, rb, cb = front(tok, w_key, w_value, w_query, w_out, norm_gain.reshape(1, -1), w_pair)
+    seq, rb, cb = front(tok, w_key, w_value, w_query, w_out, norm_gain, w_pair)
     out, seq = convolve(rb, cb, conv_weight.reshape(9 * PC, PC), seq)
     return seq.reshape(tokens.shape), out
 

time: 108 us -> 98.3 us (0.910)
  Pallas kernels: 105 us -> 97.3 us
  local copies, waits for them, and re-layouts: 1.29 us -> 0 us
    pallas_call x1, Pallas kernels: 98.7 us -> 91.1 us  [front(): pl.pallas_call(front_kernel, out_shape=(jax.ShapeDtypeStruct(tok.shape, B...]
    reshape x1 -> x0, local copies, waits for them, and re-layouts: 1.29 us -> none  [on_device(): norm_gain.reshape(1, -1)]
where the time goes in v3:
time: 98.3 us; the launch traced here: 98.1 us
  Pallas kernels  97.3 us (99%)
    pallas_call x1, Pallas kernels, front(): pl.pallas_call(front_kernel, out_shape=(jax.ShapeDtypeStruct(tok.shape, B...  91.1 us
    pallas_call x1, Pallas kernels, convolve(): pl.pallas_call(conv_kernel, out_shape=(jax.ShapeDtypeStruct((8, 8, 64, PC...  6.24 us

profile of v3, /device:TPU:1, one launch (start us, length us, event | category | flops | bytes accessed | tf_op | source)
XLA Modules:
  0.0 98.1 jit_solution(1074107191243618752)
XLA Ops:
  0.6 91.1 %front.1 = (bf16[128,1536]{1,0:T(8,128)(2,1)}, bf16[3,8,8,128]{3,2,1,0:T(8,128)(2,1)}, bf16[10,8,8,128]{3,2,1,0:T(8,128)(2,1)}) custom-call(bf16[128,1536]{1,0:T(8,128)(2,1)} %bitcast.3, bf16[192,128]{1,0:T(8,128)(2,1)} %wk.1, bf16[192,192]{1,0:T(8,128)(2,1)} %wv.1, bf16[192,512]{1,0:T(8,128)(2,1)} %wq.1, bf16[96,1536]{1,0:T(8,128)(2,1)} %wo.1, f32[1536]{0:T(1024)} %gain.1, ...), custom_call_target="tpu_custom_call" | custom-call | tf_op jit(solution)/shard_map/front/pallas_call | solution.py:518
  91.7 6.2 %convolve.1 = (bf16[8,8,64,128]{3,2,1,0:T(8,128)(2,1)}, bf16[128,1536]{1,0:T(8,128)(2,1)}) custom-call(bf16[3,8,8,128]{3,2,1,0:T(8,128)(2,1)} %get-tuple-element.7.rb, bf16[10,8,8,128]{3,2,1,0:T(8,128)(2,1)} %get-tuple-element.8.cb, bf16[1152,128]{1,0:T(8,128)(2,1)} %bitcast.4, bf16[128,1536]{1,0:T(8,128)(2,1)} %get-tuple-element.9.seq_in), custom_call_target="tpu_custom_call" | custom-call | tf_op jit(solution)/shard_map/convolve/pallas_call | solution.py:590

commit v4 on v3

v4 whole, which is shorter than its diff:
```python
import functools

import jax
import jax.numpy as jnp
from jax import lax
from jax.experimental import pallas as pl
from jax.experimental.pallas import tpu as pltpu
from jax.sharding import PartitionSpec as P

H = 4
KEY = 128
VAL = 192
PC = 128
POOL = 16
MESH = pl.DeviceIdType.MESH
BF = jnp.bfloat16
F32 = jnp.float32
BR = 320
HB = BR // 2
VMEM_LIMIT = 60 * 1024 * 1024


def coords():
    c = lax.axis_index("ctx")
    p = lax.axis_index("pair")
    return c, p, c // 32, (c // 8) % 4, (c // 2) % 4, c % 2


def ctx_of(zh, x, y, core):
    return ((zh * 4 + x) * 4 + y) * 2 + core


def at_z(c, zh, p, d):
    z = (zh * 8 + p + d + 16) % 16
    return ((z // 8) * 32 + c % 32, z % 8)


def rcopy(src, dst, ssem, rsem, dev):
    return pltpu.make_async_remote_copy(
        src_ref=src, dst_ref=dst, send_sem=ssem, recv_sem=rsem, device_id=dev, device_id_type=MESH
    )


def enter(devs):
    barrier = pltpu.get_barrier_semaphore()
    for dev in devs:
        pl.semaphore_signal(barrier, inc=1, device_id=dev, device_id_type=MESH)
    pl.semaphore_wait(barrier, len(devs))


def exchange(rb, cb, RB, CB, HM, HL, HR, rs_s, rs_r, z_s, z_r, y_s, y_r):
    c, p, zh, x, y, h = coords()
    cn, cv = (c + 1) % 64, (c + 63) % 64
    pp = [(p + k) % 8 for k in range(8)]
    yc = []
    for k in range(4):
        for e in range(2):
            if k or e:
                yc.append((ctx_of(zh, x, (y + k) % 4, (h + e) % 2), p))

    def cond(pred, fn):
        if pred is None:
            fn()
        else:
            pl.when(pred)(fn)

    tgt = c // 8
    jobs = [
        (tgt, HM, 0, None),
        (tgt + 1, HL, 1, (c % 8 == 7) & (tgt < 7)),
        (tgt - 1, HR, 2, (c % 8 == 0) & (tgt > 0)),
    ]

    for t, buf, b, pred in jobs:
        for f in (1, 0):
            for k in (2, 1, 3, 0):
                dc = ctx_of(zh if f == 0 else 1 - zh, (x + k) % 4, y, h)

                def go(t=t, buf=buf, b=b, dc=dc):
                    send(cb, buf.at[p], z_s.at[b], z_r.at[b], (dc, t))

                if f or k:
                    cond(pred, go)
                else:
                    away = t != p
                    cond(away if pred is None else away & pred, go)

    for b, dc, pred in ((0, cn, c < 63), (2, cv, c > 0)):

        @pl.when(pred)
        def _():
            for k in range(8):
                send(rb, RB.at[b, p], rs_s.at[b], rs_r.at[b], (dc, pp[k]))

    for k in range(1, 8):
        send(rb, RB.at[1, p], rs_s.at[1], rs_r.at[1], (c, pp[k]))
    RB[1, pl.ds(p, 1)] = rb[...].reshape(1, 8, PC)
    for t, buf, b, pred in jobs:

        @pl.when((t == p) if pred is None else (t == p) & pred)
        def _():
            buf[pl.ds(p, 1)] = cb[...].reshape(1, 8, PC)

    @pl.when(c == 0)
    def _():
        RB[0] = jnp.zeros((8, 8, PC), BF)

    @pl.when(c == 63)
    def _():
        RB[2] = jnp.zeros((8, 8, PC), BF)

    @pl.when(p == 0)
    def _():
        CB[0] = jnp.zeros((8, 8, PC), BF)

    @pl.when(p == 7)
    def _():
        CB[9] = jnp.zeros((8, 8, PC), BF)

    mine = 1 + 2 * y + h
    spreads = (
        (HM, 0, p, None, mine),
        (HL, 1, p - 1, (y == 3) & (h == 1) & (p > 0), 0),
        (HR, 2, p + 1, (y == 0) & (h == 0) & (p < 7), 9),
    )
    for buf, b, owner, member, cslot in spreads:

        def take(buf=buf, b=b, owner=owner, cslot=cslot):
            inside = (zh == owner // 4) & (x == owner % 4)
            pl.when(inside)(lambda: received(buf.at[pl.ds(0, 7)], z_r.at[b]))
            pl.when(jnp.logical_not(inside))(lambda: received(buf, z_r.at[b]))
            for k in range(7):
                send(buf, CB.at[cslot], y_s.at[b], y_r.at[b], yc[k])
            CB[pl.ds(cslot, 1)] = buf[...].reshape(1, 8, 8, PC)

        cond(member, take)

    received(CB.at[pl.ds(1, 7)], y_r.at[0])

    @pl.when((p > 0) & jnp.logical_not((y == 3) & (h == 1)))
    def _():
        received(CB.at[0], y_r.at[1])

    @pl.when((p < 7) & jnp.logical_not((y == 0) & (h == 0)))
    def _():
        received(CB.at[9], y_r.at[2])

    received(RB.at[1, pl.ds(0, 7)], rs_r.at[1])
    drained(RB.at[1, pl.ds(0, 7)], rs_s.at[1])
    for b, came, went in ((0, c > 0, c < 63), (2, c < 63, c > 0)):
        pl.when(came)(lambda b=b: received(RB.at[b], rs_r.at[b]))
        pl.when(went)(lambda b=b: drained(RB.at[b], rs_s.at[b]))
    for t, buf, b, pred in jobs:

        def gone(t=t, buf=buf, b=b):
            pl.when(t == p)(lambda: drained(buf.at[pl.ds(0, 7)], z_s.at[b]))
            pl.when(t != p)(lambda: drained(buf, z_s.at[b]))

        cond(pred, gone)
    for buf, b, owner, member, cslot in spreads:
        cond(member, lambda b=b: drained(CB.at[pl.ds(0, 7)], y_s.at[b]))


def send(src, dst, s, r, dev):
    rcopy(src, dst, s, r, dev).start()


def received(ref, sem):
    rcopy(ref, ref, sem, sem, (0, 0)).wait_recv()


def drained(ref, sem):
    rcopy(ref, ref, sem, sem, (0, 0)).wait_send()


DIST = (1, -1, 2, -2, 3, -3, 4)


class Weights:
    def __init__(self, arrs, place, ss, zr, nr, pr):
        self.arrs = arrs
        self.c, self.p, self.zh, x, y, self.h = place
        self.color = (x + y) % 2
        self.partner = (self.c + 1 - 2 * self.h, self.p)
        self.plane = [
            (ctx_of(self.zh, (x + dx) % 4, (y + dy) % 4, self.h), self.p)
            for dx, dy in ((1, 0), (3, 0), (0, 1), (0, 3))
        ]
        self.ss, self.zr, self.nr, self.pr = ss, zr, nr, pr

    def at(self, d):
        return at_z(self.c, self.zh, self.p, d)

    def quarter(self, i, base, h, color, side=None):
        src, _ = self.arrs[i]
        r, w = src.shape
        if i < 3:
            n = r // 4
            row, lane, wide = base + h * 2 * n + color * n, 0, w
        else:
            n = r // 2
            row, lane, wide = base + h * n, pl.multiple_of(color * (w // 2), w // 2), w // 2
        if side is not None:
            wide = wide // 2
            lane = lane + side * wide
            if i == 3:
                lane = pl.multiple_of(lane, wide)
        return pl.ds(pl.multiple_of(row, n), n), pl.ds(lane, wide)

    def own(self, i, side=None):
        rows, lanes = self.quarter(i, 0, self.h, self.color, side)
        return self.arrs[i][0].at[rows, lanes]

    def part(self, i, m, flip_h=0, flip_c=0, side=None, d=None):
        src, out = self.arrs[i]
        d = DIST[m] if d is None else d
        base = ((self.p - d + 8) % 8) * src.shape[0]
        h = 1 - self.h if flip_h else self.h
        color = 1 - self.color if flip_c else self.color
        rows, lanes = self.quarter(i, base, h, color, side)
        return out.at[rows, lanes]

    def first(self, i):
        for di, d in enumerate((1, -1)):
            dst = self.part(i, di, d=0)
            send(self.own(i), dst, self.ss.at[i], self.zr.at[i, di], self.at(d))

    def hop(self, i, t):
        for di, d in enumerate((1, -1)):
            m = (t - 1) * 2 + di
            received(self.part(i, m), self.zr.at[i, m])
            if t < 3 or i >= 2 or i == di:
                ref = self.part(i, m, side=di if t == 3 and i >= 2 else None)
                send(ref, ref, self.ss.at[i], self.zr.at[i, min(m + 2, 6)], self.at(d))
            self.spread(i, m)

    def spread(self, i, m):
        ref = self.part(i, m)
        send(ref, ref, self.ss.at[i], self.pr.at[i], self.partner)
        to = self.plane[m % 4]
        send(ref, ref, self.ss.at[i], self.nr.at[i, m], to)

    def take(self, i, m):
        received(self.part(i, m), self.zr.at[i, m])
        self.spread(i, m)

    def near(self, i):
        for m in range(7):
            ref = self.part(i, m, flip_c=1)
            received(ref, self.nr.at[i, m])
            send(ref, ref, self.ss.at[i], self.pr.at[i], self.partner)

    def done(self, i):
        src, out = self.arrs[i]
        received(out.at[pl.ds(0, 7 * src.shape[0] // 2), :], self.pr.at[i])

    def finish(self):
        for i, (src, out) in enumerate(self.arrs):
            drained(out.at[pl.ds(0, 7 * src.shape[0]), :], self.ss.at[i])


class Gather:
    def __init__(self, kv, place, ss, rs, pr):
        self.kv = kv
        c, p, zh, x, y, h = place
        self.ss, self.rs, self.pr = ss, rs, pr
        self.partner = (c + 1 - 2 * h, p)
        self.ap = (ctx_of(zh, (x + 1 - h) % 4, (y + h) % 4, h), p)
        self.am = (ctx_of(zh, (x + 3 + h) % 4, (y + 4 - h) % 4, h), p)
        self.af = (ctx_of(zh, (x + 2 - 2 * h) % 4, (y + 2 * h) % 4, h), p)
        self.bp = (ctx_of(zh, (x + h) % 4, (y + 1 - h) % 4, h), p)
        self.bm = (ctx_of(zh, (x + 4 - h) % 4, (y + 3 + h) % 4, h), p)

    def slot(self, g, j, m, r=0):
        return self.kv.at[((g * 4 + j) * 2 + r) * 4 + m]

    def half(self, g, j, m, k):
        return self.kv.at[((g * 4 + j) * 2) * 4 + m, pl.ds(k * HB, HB), :]

    def got(self, ref, k):
        received(ref, self.rs.at[k])

    def send(self, src, dst, k, dev):
        send(src, dst, self.ss, self.rs.at[k], dev)

    def to_b(self, g, j, src=None):
        src = self.slot(g, j, 0) if src is None else src
        k = 15 * g + 3 + 3 * j
        self.send(src, self.slot(g, j, 1), k, self.bp)
        self.send(src, self.slot(g, j, 2), k + 1, self.bm)

    def to_partner(self, g, j, m, src=None):
        src = self.slot(g, j, m) if src is None else src
        send(src, self.slot(g, j, m, 1), self.ss, self.pr.at[4 * g + j], self.partner)

    def own(self, g, src=None):
        a = self.slot(g, 0, 0) if src is None else src
        self.send(a, self.slot(g, 1, 0), 15 * g, self.ap)
        self.send(a, self.slot(g, 2, 0), 15 * g + 1, self.am)
        self.send(a, self.slot(g, 3, 0), 15 * g + 2, self.af)
        self.to_b(g, 0, src)
        self.to_partner(g, 0, 0, src)

    def a_near(self, g):
        for j, k in ((1, 0), (2, 1)):
            self.got(self.slot(g, j, 0), 15 * g + k)
            self.to_b(g, j)
            self.to_partner(g, j, 0)

    def a_far(self, g):
        self.got(self.slot(g, 3, 0), 15 * g + 2)
        self.to_b(g, 3)
        self.to_partner(g, 3, 0)

    def b_near(self, g, j):
        base = 15 * g + 3 + 3 * j
        for m, k, dev in ((1, 0, self.bp), (2, 1, self.bm)):
            self.got(self.slot(g, j, m), base + k)
            self.send(self.half(g, j, m, k), self.half(g, j, 3, k), base + 2, dev)
            self.to_partner(g, j, m)

    def b_far(self, g, j):
        self.got(self.slot(g, j, 3), 15 * g + 3 + 3 * j + 2)
        self.to_partner(g, j, 3)

    def from_partner(self, g, j):
        received(self.kv.at[pl.ds(((g * 4 + j) * 2 + 1) * 4, 4)], self.pr.at[4 * g + j])

    def finish(self):
        drained(self.kv, self.ss)


def front_kernel(
    tok_hbm, wk, wv, wq, wo, gain, wpair_hbm,
    seq, RB, CB,
    WK, WV, WQ, WO, tok, wpair, kv, blk, relay, q, acc, high, mixed, rb, cb, HM, HL, HR,
    wss, wzr, wnr, wpr, kss, krs, kpr, zr, hr, ls, rs_s, rs_r, z_s, z_r, y_s, y_r,
):
    place = coords()
    c, p, zh, x, y, h = place
    arrs = ((wk, WK), (wv, WV), (wq, WQ), (wo, WO))
    ring = Weights(arrs, place, wss, wzr, wnr, wpr)
    kvs = Gather(kv, place, kss, krs, kpr)
    enter([ring.at(1), ring.at(-1), ring.partner] + ring.plane)
    for i in range(3):
        ring.first(i)
    locs = []
    for i, (src, out) in enumerate(arrs):
        r = src.shape[0]
        locs.append((src, out.at[pl.ds(pl.multiple_of(p * r, r), r), :]))
    locs += [(tok_hbm, tok), (wpair_hbm, wpair)]
    locs = [pltpu.make_async_copy(src, dst, ls.at[i]) for i, (src, dst) in enumerate(locs)]
    for cp in locs:
        cp.start()

    for n in (1, 2, 3):
        for i in range(3):
            ring.hop(i, n)
    ring.take(0, 6)
    ring.take(1, 6)
    for i in (0, 1, 4):
        locs[i].wait()
    ring.near(0)
    ring.near(1)
    ring.take(2, 6)
    ring.done(0)
    ring.done(1)
    t = tok[...]
    blk[0:128, :] = jnp.dot(t, WK[...], preferred_element_type=F32).astype(BF)
    v = jnp.dot(t, WV[...], preferred_element_type=F32)
    blk[128:256, :] = v[:, :128].astype(BF)
    blk[256:320, :] = jnp.concatenate([v[0:64, 128:192], v[64:128, 128:192]], axis=1).astype(BF)

    for k in range(2):
        send(blk.at[pl.ds(k * HB, HB), :], relay.at[k], kss, hr.at[k], ring.at((4, -4)[k]))
    kvs.own(0, blk)
    loc = pltpu.make_async_copy(blk, kvs.slot(0, 0, 0), ls.at[6])
    loc.start()
    acc[...] = jnp.zeros_like(acc)
    high[...] = jnp.full_like(high, -1e30)
    kvs.a_near(0)
    kvs.a_far(0)
    ring.near(2)
    kvs.b_near(0, 0)
    for k in range(2):
        received(relay.at[k], hr.at[k])
        send(relay.at[k], kvs.half(1, 0, 0, k), kss, zr, ring.at((4, -4)[k]))
    ring.first(3)
    kvs.b_near(0, 1)
    kvs.b_near(0, 2)
    kvs.b_far(0, 0)
    kvs.b_near(0, 3)
    loc.wait()
    locs[2].wait()
    ring.done(2)
    qq = jnp.dot(tok[...], WQ[...], preferred_element_type=F32).astype(BF)
    for n in range(H):
        q[n * 128 : (n + 1) * 128, :] = qq[:, n * KEY : (n + 1) * KEY]
    ring.hop(3, 1)
    for j in (1, 2, 3):
        kvs.b_far(0, j)
    received(kvs.slot(1, 0, 0), zr)
    kvs.own(1)

    scale = KEY ** (-0.5) * 1.4426950408889634

    def attend(g, j):
        kvs.from_partner(g, j)
        part = kv[pl.ds((g * 4 + j) * 8, 8)]
        k = part[:, 0:128, :].reshape(1024, 128)
        v1 = part[:, 128:256, :].reshape(1024, 128)
        lo = part[:, 256:320, :].astype(F32)
        hi = pltpu.roll(lo.reshape(512, 128), 64, 1).reshape(8, 64, 128)
        v2 = jnp.concatenate([lo, hi], axis=1).reshape(1024, 128)
        lane = lax.broadcasted_iota(jnp.int32, (1024, 128), 1)
        v2 = jnp.where(lane == 64, 1.0, v2).astype(BF)
        m = high[:, 0:1]
        s = lax.dot_general(q[...], k, (((1,), (1,)), ((), ())), preferred_element_type=F32)
        m2 = jnp.maximum(m, jnp.max(s, axis=1, keepdims=True))
        w = jnp.exp2((s - m2) * scale).astype(BF)
        o = jnp.dot(w, jnp.concatenate([v1, v2], axis=1), preferred_element_type=F32)
        acc[...] = acc[...] * jnp.exp2((m - m2) * scale) + o
        high[...] = jnp.broadcast_to(m2, high.shape)

    attend(0, 0)
    ring.hop(3, 2)
    kvs.a_near(1)
    kvs.a_far(1)
    kvs.b_near(1, 0)
    attend(0, 1)
    ring.hop(3, 3)
    kvs.b_near(1, 1)
    kvs.b_near(1, 2)
    kvs.b_far(1, 0)
    attend(0, 2)
    ring.take(3, 6)
    kvs.b_near(1, 3)
    kvs.b_far(1, 1)
    kvs.b_far(1, 2)
    attend(0, 3)
    ring.near(3)
    kvs.b_far(1, 3)
    for j in range(4):
        attend(1, j)
    locs[3].wait()
    locs[5].wait()
    ring.done(3)

    a = acc[...]
    mx = (a[:, 0:VAL] / a[:, VAL : VAL + 1]).astype(BF)
    for n in range(H):
        mixed[:, n * VAL : (n + 1) * VAL] = mx[n * 128 : (n + 1) * 128, :]
    summed = tok[...].astype(F32) + jnp.dot(mixed[...], WO[...], preferred_element_type=F32)
    seq[...] = summed.astype(BF)
    pooled = jnp.mean(summed.reshape(8, POOL, summed.shape[1]), axis=1)
    ms = jnp.mean(pooled * pooled, axis=-1, keepdims=True)
    normed = (pooled * lax.rsqrt(ms + 1e-06) * gain[...].reshape(1, -1)).astype(BF)
    both = jnp.dot(normed, wpair[...], preferred_element_type=F32).astype(BF)
    rb[...] = both[:, :PC]
    cb[...] = both[:, PC:]
    exchange(rb, cb, RB, CB, HM, HL, HR, rs_s, rs_r, z_s, z_r, y_s, y_r)
    ring.finish()
    kvs.finish()


def front(tok, wk, wv, wq, wo, gain, wpair):
    vm = pl.BlockSpec(memory_space=pltpu.VMEM)
    dma = pltpu.SemaphoreType.DMA
    hold = pltpu.VMEM((8, 8, PC), BF)
    hbm = pl.BlockSpec(memory_space=pl.ANY)
    return pl.pallas_call(
        front_kernel,
        out_shape=(
            jax.ShapeDtypeStruct(tok.shape, BF),
            jax.ShapeDtypeStruct((3, 8, 8, PC), BF),
            jax.ShapeDtypeStruct((10, 8, 8, PC), BF),
        ),
        in_specs=[hbm] * 5 + [vm, hbm],
        out_specs=(vm,) * 3,
        scratch_shapes=[pltpu.VMEM((8 * w.shape[0], w.shape[1]), BF) for w in (wk, wv, wq, wo)]
        + [
            pltpu.VMEM(tok.shape, BF),
            pltpu.VMEM(wpair.shape, BF),
            pltpu.VMEM((64, BR, 128), BF),
            pltpu.VMEM((BR, 128), BF),
            pltpu.VMEM((2, HB, 128), BF),
            pltpu.VMEM((512, 128), BF),
            pltpu.VMEM((512, 256), F32),
            pltpu.VMEM((512, 128), F32),
            pltpu.VMEM((128, H * VAL), BF),
            pltpu.VMEM((8, PC), BF),
            pltpu.VMEM((8, PC), BF),
            hold,
            hold,
            hold,
        ]
        + [dma((4,)), dma((4, 7)), dma((4, 7)), dma((4,)), dma, dma((30,)), dma((8,)), dma, dma((2,)), dma((7,))]
        + [dma((3,))] * 6,
        compiler_params=pltpu.CompilerParams(
            collective_id=0, has_side_effects=True, vmem_limit_bytes=VMEM_LIMIT
        ),
        name="front",
    )(tok, wk, wv, wq, wo, gain, wpair)


def conv_kernel(rb, cb, w, seq_in, out, seq_out, tile, line, wide, sems):
    bring = pltpu.make_async_copy(seq_in, line, sems.at[8])
    bring.start()

    for r in range(4):
        for n in range(2):
            a = r - n
            for b in range(3):
                k = (3 * r + b) * PC
                if 0 <= a < 3:
                    tap = (3 * a + b) * PC
                    wide[k : k + PC, n * PC : (n + 1) * PC] = w[tap : tap + PC, :]
                else:
                    wide[k : k + PC, n * PC : (n + 1) * PC] = jnp.zeros((PC, PC), BF)

    def put(s):
        return pltpu.make_async_copy(tile.at[s], out.at[s], sems.at[s])

    first = (0, 4, 1, 5)

    def seq(s):
        prev = rb[0, pl.ds(s, 1)].reshape(8, PC).astype(F32)
        own = rb[1, pl.ds(s, 1)].reshape(8, PC).astype(F32)
        nxt = rb[2, pl.ds(s, 1)].reshape(8, PC).astype(F32)
        col = jnp.concatenate([cb[k, pl.ds(s, 1)].reshape(8, PC) for k in range(10)], axis=0).astype(F32)
        rows = [prev[6:7], prev[7:8]] + [own[k : k + 1] for k in range(8)] + [nxt[0:1], nxt[1:2]]
        shifted = [col[6 + 2 * b : 70 + 2 * b] for b in range(3)]
        maps = [[(r * cs).astype(BF) for r in rows] for cs in shifted]
        lhs = jnp.concatenate(
            [
                jnp.concatenate([maps[b][i + 2 * r] for i in first], axis=0)
                for r in range(4)
                for b in range(3)
            ],
            axis=1,
        )
        t = jnp.dot(lhs, wide[...], preferred_element_type=F32)
        for q, i in enumerate(first):
            for n in range(2):
                conv = t[64 * q : 64 * q + 64, n * PC : (n + 1) * PC]
                res = maps[1][i + 2 * n + 2].astype(F32) + jax.nn.gelu(conv)
                tile[pl.ds(s, 1), i + 2 * n] = res.astype(BF).reshape(1, 64, PC)
        put(s).start()

    def two(n, carry):
        seq(2 * n)
        seq(2 * n + 1)
        return carry

    lax.fori_loop(0, 4, two, 0)
    bring.wait()
    give = pltpu.make_async_copy(line, seq_out, sems.at[8])
    give.start()
    for s in range(8):
        put(s).wait()
    give.wait()


def convolve(rb, cb, w, seq):
    vm = pl.BlockSpec(memory_space=pltpu.VMEM)
    hbm = pl.BlockSpec(memory_space=pl.ANY)
    return pl.pallas_call(
        conv_kernel,
        out_shape=(jax.ShapeDtypeStruct((8, 8, 64, PC), BF), jax.ShapeDtypeStruct(seq.shape, BF)),
        in_specs=[vm] * 3 + [hbm],
        out_specs=(hbm, hbm),
        scratch_shapes=[
            pltpu.VMEM((8, 8, 64, PC), BF),
            pltpu.VMEM(seq.shape, BF),
            pltpu.VMEM((12 * PC, 2 * PC), BF),
            pltpu.SemaphoreType.DMA((9,)),
        ],
        compiler_params=pltpu.CompilerParams(vmem_limit_bytes=VMEM_LIMIT),
        name="convolve",
    )(rb, cb, w, seq)


def on_device(tokens, w_query, w_key, w_value, w_out, norm_gain, w_pair, conv_weight):
    tok = tokens.reshape(tokens.shape[1], tokens.shape[2])
    seq, rb, cb = front(tok, w_key, w_value, w_query, w_out, norm_gain, w_pair)
    out, seq = convolve(rb, cb, conv_weight.reshape(9 * PC, PC), seq)
    return seq.reshape(tokens.shape), out


def solution(mesh):
    return jax.shard_map(
        on_device,
        mesh=mesh,
        in_specs=(
            P("pair", "ctx", None),
            P("pair", None),
            P("pair", None),
            P("pair", None),
            P("pair", None),
            P(),
            P(),
            P(),
        ),
        out_specs=(P("pair", "ctx", None), P(None, "ctx", "pair", None)),
        check_vma=False,
    )
```

time: 98.3 us -> 88.7 us (0.902)
  Pallas kernels: 97.3 us -> 87.8 us
    pallas_call x1, Pallas kernels: 91.1 us -> 82.8 us  [front(): pl.pallas_call(front_kernel, out_shape=(jax.ShapeDtypeStruct(tok.shape, B...]
    pallas_call x1, Pallas kernels: 6.24 us -> 5 us  [convolve(): pl.pallas_call(conv_kernel, out_shape=(jax.ShapeDtypeStruct((8, 8, 64, PC...]
where the time goes in v4:
time: 88.7 us; the launch traced here: 88.5 us
  Pallas kernels  87.8 us (99%)
    pallas_call x1, Pallas kernels, front(): pl.pallas_call(front_kernel, out_shape=(jax.ShapeDtypeStruct(tok.shape, B...  82.8 us
    pallas_call x1, Pallas kernels, convolve(): pl.pallas_call(conv_kernel, out_shape=(jax.ShapeDtypeStruct((8, 8, 64, PC...  5 us

profile of v4, /device:TPU:1, one launch (start us, length us, event | category | flops | bytes accessed | tf_op | source)
XLA Modules:
  0.0 88.5 jit_solution(16718743040205437491)
XLA Ops:
  0.6 82.8 %front.1 = (bf16[128,1536]{1,0:T(8,128)(2,1)}, bf16[3,8,8,128]{3,2,1,0:T(8,128)(2,1)}, bf16[10,8,8,128]{3,2,1,0:T(8,128)(2,1)}) custom-call(bf16[128,1536]{1,0:T(8,128)(2,1)} %bitcast.3, bf16[192,128]{1,0:T(8,128)(2,1)} %wk.1, bf16[192,192]{1,0:T(8,128)(2,1)} %wv.1, bf16[192,512]{1,0:T(8,128)(2,1)} %wq.1, bf16[96,1536]{1,0:T(8,128)(2,1)} %wo.1, f32[1536]{0:T(1024)} %gain.1, ...), custom_call_target="tpu_custom_call" | custom-call | tf_op jit(solution)/shard_map/front/pallas_call | solution.py:471
  83.5 5.0 %convolve.1 = (bf16[8,8,64,128]{3,2,1,0:T(8,128)(2,1)}, bf16[128,1536]{1,0:T(8,128)(2,1)}) custom-call(bf16[3,8,8,128]{3,2,1,0:T(8,128)(2,1)} %get-tuple-element.7.rb, bf16[10,8,8,128]{3,2,1,0:T(8,128)(2,1)} %get-tuple-element.8.cb, bf16[1152,128]{1,0:T(8,128)(2,1)} %bitcast.4, bf16[128,1536]{1,0:T(8,128)(2,1)} %get-tuple-element.9.seq_in), custom_call_target="tpu_custom_call" | custom-call | tf_op jit(solution)/shard_map/convolve/pallas_call | solution.py:567

commit v5 on v4

--- a/solution.py
+++ b/solution.py
@@ -220,6 +220,12 @@
         rows, lanes = self.quarter(i, base, h, color, side)
         return out.at[rows, lanes]
 
+    def direct(self):
+        for m in range(7):
+            for i in range(2):
+                d = DIST[m] if m < 6 else (4, -4)[i]
+                send(self.own(i), self.part(i, m, d=0), self.ss.at[i], self.zr.at[i, m], self.at(d))
+
     def first(self, i):
         for di, d in enumerate((1, -1)):
             dst = self.part(i, di, d=0)
@@ -229,9 +235,8 @@
         for di, d in enumerate((1, -1)):
             m = (t - 1) * 2 + di
             received(self.part(i, m), self.zr.at[i, m])
-            if t < 3 or i >= 2 or i == di:
-                ref = self.part(i, m, side=di if t == 3 and i >= 2 else None)
-                send(ref, ref, self.ss.at[i], self.zr.at[i, min(m + 2, 6)], self.at(d))
+            ref = self.part(i, m, side=di if t == 3 else None)
+            send(ref, ref, self.ss.at[i], self.zr.at[i, min(m + 2, 6)], self.at(d))
             self.spread(i, m)
 
     def spread(self, i, m):
@@ -293,10 +298,13 @@
         src = self.slot(g, j, m) if src is None else src
         send(src, self.slot(g, j, m, 1), self.ss, self.pr.at[4 * g + j], self.partner)
 
-    def own(self, g, src=None):
+    def own_a(self, g, src=None):
         a = self.slot(g, 0, 0) if src is None else src
         self.send(a, self.slot(g, 1, 0), 15 * g, self.ap)
         self.send(a, self.slot(g, 2, 0), 15 * g + 1, self.am)
+
+    def own_b(self, g, src=None):
+        a = self.slot(g, 0, 0) if src is None else src
         self.send(a, self.slot(g, 3, 0), 15 * g + 2, self.af)
         self.to_b(g, 0, src)
         self.to_partner(g, 0, 0, src)
@@ -333,7 +341,7 @@
 def front_kernel(
     tok_hbm, wk, wv, wq, wo, gain, wpair_hbm,
     seq, RB, CB,
-    WK, WV, WQ, WO, tok, wpair, kv, blk, relay, q, acc, high, mixed, rb, cb, HM, HL, HR,
+    WK, WV, WQ, WO, tok, wpair, kv, blk, relay, q, acc, high, mixed, line, rb, cb, HM, HL, HR,
     wss, wzr, wnr, wpr, kss, krs, kpr, zr, hr, ls, rs_s, rs_r, z_s, z_r, y_s, y_r,
 ):
     place = coords()
@@ -341,9 +349,9 @@
     arrs = ((wk, WK), (wv, WV), (wq, WQ), (wo, WO))
     ring = Weights(arrs, place, wss, wzr, wnr, wpr)
     kvs = Gather(kv, place, kss, krs, kpr)
-    enter([ring.at(1), ring.at(-1), ring.partner] + ring.plane)
-    for i in range(3):
-        ring.first(i)
+    enter([ring.at(d) for d in (4, -4, 3, -3, 2, -2, 1, -1)] + ring.plane + [ring.partner])
+    ring.direct()
+    ring.first(2)
     locs = []
     for i, (src, out) in enumerate(arrs):
         r = src.shape[0]
@@ -353,16 +361,16 @@
     for cp in locs:
         cp.start()
 
-    for n in (1, 2, 3):
-        for i in range(3):
-            ring.hop(i, n)
-    ring.take(0, 6)
-    ring.take(1, 6)
+    for m in range(7):
+        ring.take(0, m)
+        ring.take(1, m)
+        if m == 3:
+            ring.hop(2, 1)
     for i in (0, 1, 4):
         locs[i].wait()
     ring.near(0)
     ring.near(1)
-    ring.take(2, 6)
+    ring.hop(2, 2)
     ring.done(0)
     ring.done(1)
     t = tok[...]
@@ -371,36 +379,38 @@
     blk[128:256, :] = v[:, :128].astype(BF)
     blk[256:320, :] = jnp.concatenate([v[0:64, 128:192], v[64:128, 128:192]], axis=1).astype(BF)
 
+    kvs.own_a(0, blk)
     for k in range(2):
         send(blk.at[pl.ds(k * HB, HB), :], relay.at[k], kss, hr.at[k], ring.at((4, -4)[k]))
-    kvs.own(0, blk)
+    kvs.own_b(0, blk)
+    ring.first(3)
     loc = pltpu.make_async_copy(blk, kvs.slot(0, 0, 0), ls.at[6])
     loc.start()
     acc[...] = jnp.zeros_like(acc)
     high[...] = jnp.full_like(high, -1e30)
     kvs.a_near(0)
+    ring.hop(2, 3)
     kvs.a_far(0)
-    ring.near(2)
     kvs.b_near(0, 0)
     for k in range(2):
         received(relay.at[k], hr.at[k])
         send(relay.at[k], kvs.half(1, 0, 0, k), kss, zr, ring.at((4, -4)[k]))
-    ring.first(3)
+    ring.hop(3, 1)
     kvs.b_near(0, 1)
     kvs.b_near(0, 2)
     kvs.b_far(0, 0)
+    ring.take(2, 6)
     kvs.b_near(0, 3)
+    received(kvs.slot(1, 0, 0), zr)
+    kvs.own_a(1)
+    kvs.own_b(1)
+    ring.near(2)
     loc.wait()
     locs[2].wait()
     ring.done(2)
     qq = jnp.dot(tok[...], WQ[...], preferred_element_type=F32).astype(BF)
     for n in range(H):
         q[n * 128 : (n + 1) * 128, :] = qq[:, n * KEY : (n + 1) * KEY]
-    ring.hop(3, 1)
-    for j in (1, 2, 3):
-        kvs.b_far(0, j)
-    received(kvs.slot(1, 0, 0), zr)
-    kvs.own(1)
 
     scale = KEY ** (-0.5) * 1.4426950408889634
 
@@ -424,24 +434,28 @@
 
     attend(0, 0)
     ring.hop(3, 2)
+    for j in (1, 2, 3):
+        kvs.b_far(0, j)
     kvs.a_near(1)
     kvs.a_far(1)
     kvs.b_near(1, 0)
     attend(0, 1)
     ring.hop(3, 3)
+    attend(0, 2)
     kvs.b_near(1, 1)
     kvs.b_near(1, 2)
     kvs.b_far(1, 0)
-    attend(0, 2)
+    attend(0, 3)
     ring.take(3, 6)
     kvs.b_near(1, 3)
     kvs.b_far(1, 1)
     kvs.b_far(1, 2)
-    attend(0, 3)
+    attend(1, 0)
+    kvs.b_far(1, 3)
+    attend(1, 1)
     ring.near(3)
-    kvs.b_far(1, 3)
-    for j in range(4):
-        attend(1, j)
+    attend(1, 2)
+    attend(1, 3)
     locs[3].wait()
     locs[5].wait()
     ring.done(3)
@@ -451,7 +465,9 @@
     for n in range(H):
         mixed[:, n * VAL : (n + 1) * VAL] = mx[n * 128 : (n + 1) * 128, :]
     summed = tok[...].astype(F32) + jnp.dot(mixed[...], WO[...], preferred_element_type=F32)
-    seq[...] = summed.astype(BF)
+    line[...] = summed.astype(BF)
+    keep = pltpu.make_async_copy(line, seq, ls.at[7])
+    keep.start()
     pooled = jnp.mean(summed.reshape(8, POOL, summed.shape[1]), axis=1)
     ms = jnp.mean(pooled * pooled, axis=-1, keepdims=True)
     normed = (pooled * lax.rsqrt(ms + 1e-06) * gain[...].reshape(1, -1)).astype(BF)
@@ -461,6 +477,7 @@
     exchange(rb, cb, RB, CB, HM, HL, HR, rs_s, rs_r, z_s, z_r, y_s, y_r)
     ring.finish()
     kvs.finish()
+    keep.wait()
 
 
 def front(tok, wk, wv, wq, wo, gain, wpair):
@@ -476,7 +493,7 @@
             jax.ShapeDtypeStruct((10, 8, 8, PC), BF),
         ),
         in_specs=[hbm] * 5 + [vm, hbm],
-        out_specs=(vm,) * 3,
+        out_specs=(hbm, vm, vm),
         scratch_shapes=[pltpu.VMEM((8 * w.shape[0], w.shape[1]), BF) for w in (wk, wv, wq, wo)]
         + [
             pltpu.VMEM(tok.shape, BF),
@@ -488,13 +505,14 @@
             pltpu.VMEM((512, 256), F32),
             pltpu.VMEM((512, 128), F32),
             pltpu.VMEM((128, H * VAL), BF),
+            pltpu.VMEM(tok.shape, BF),
             pltpu.VMEM((8, PC), BF),
             pltpu.VMEM((8, PC), BF),
             hold,
             hold,
             hold,
         ]
-        + [dma((4,)), dma((4, 7)), dma((4, 7)), dma((4,)), dma, dma((30,)), dma((8,)), dma, dma((2,)), dma((7,))]
+        + [dma((4,)), dma((4, 7)), dma((4, 7)), dma((4,)), dma, dma((30,)), dma((8,)), dma, dma((2,)), dma((8,))]
         + [dma((3,))] * 6,
         compiler_params=pltpu.CompilerParams(
             collective_id=0, has_side_effects=True, vmem_limit_bytes=VMEM_LIMIT

time: 88.7 us -> 85.2 us (0.961)
  Pallas kernels: 87.8 us -> 84.3 us
    pallas_call x1, Pallas kernels: 82.8 us -> 79.3 us  [front(): pl.pallas_call(front_kernel, out_shape=(jax.ShapeDtypeStruct(tok.shape, B...]
where the time goes in v5:
time: 85.2 us; the launch traced here: 85 us
  Pallas kernels  84.3 us (99%)
    pallas_call x1, Pallas kernels, front(): pl.pallas_call(front_kernel, out_shape=(jax.ShapeDtypeStruct(tok.shape, B...  79.3 us
    pallas_call x1, Pallas kernels, convolve(): pl.pallas_call(conv_kernel, out_shape=(jax.ShapeDtypeStruct((8, 8, 64, PC...  5 us

profile of v5, /device:TPU:1, one launch (start us, length us, event | category | flops | bytes accessed | tf_op | source)
XLA Modules:
  0.0 85.0 jit_solution(296119288020587915)
XLA Ops:
  0.6 79.3 %front.1 = (bf16[128,1536]{1,0:T(8,128)(2,1)}, bf16[3,8,8,128]{3,2,1,0:T(8,128)(2,1)}, bf16[10,8,8,128]{3,2,1,0:T(8,128)(2,1)}) custom-call(bf16[128,1536]{1,0:T(8,128)(2,1)} %bitcast.3, bf16[192,128]{1,0:T(8,128)(2,1)} %wk.1, bf16[192,192]{1,0:T(8,128)(2,1)} %wv.1, bf16[192,512]{1,0:T(8,128)(2,1)} %wq.1, bf16[96,1536]{1,0:T(8,128)(2,1)} %wo.1, f32[1536]{0:T(1024)} %gain.1, ...), custom_call_target="tpu_custom_call" | custom-call | tf_op jit(solution)/shard_map/front/pallas_call | solution.py:488
  80.0 5.0 %convolve.1 = (bf16[8,8,64,128]{3,2,1,0:T(8,128)(2,1)}, bf16[128,1536]{1,0:T(8,128)(2,1)}) custom-call(bf16[3,8,8,128]{3,2,1,0:T(8,128)(2,1)} %get-tuple-element.7.rb, bf16[10,8,8,128]{3,2,1,0:T(8,128)(2,1)} %get-tuple-element.8.cb, bf16[1152,128]{1,0:T(8,128)(2,1)} %bitcast.4, bf16[128,1536]{1,0:T(8,128)(2,1)} %get-tuple-element.9.seq_in), custom_call_target="tpu_custom_call" | custom-call | tf_op jit(solution)/shard_map/convolve/pallas_call | solution.py:585
